TPU v7x, 32 devices: a whole 2x2x4 slice. The times are simulated.
32 devices in a mesh: groups: 2 (over y), ctx: 8 (over z, core), heads: 2 (over x), rep: 1.
Axes of the slice: x: 2, y: 2, z: 4, core: 2. Of those that a mesh axis runs over, the one named last changes fastest.
Arguments:
- queries: bfloat16 [2048, 512], P(('groups', 'ctx'), ('heads', 'rep')), parts along dimension 0, may hold values from -2 to 2
- keys: bfloat16 [2048, 512], P(('groups', 'ctx'), ('heads', 'rep')), parts along dimension 0, may hold values from -2 to 2
- values: bfloat16 [2048, 512], P(('groups', 'ctx'), ('heads', 'rep')), parts along dimension 0, may hold values from -6 to 6
- doc_ids: int32 [2048], P(('groups', 'ctx')), parts along dimension 0, may hold values from 0 to 3, never falling along the last dimension, each value on 1 to 512 neighbouring positions
Outputs:
- attended: bfloat16 [2048, 512], P(('groups', 'ctx'), ('heads', 'rep')), parts along dimension 0
There are 2 independent parts, one for each index of `groups`. A program takes and returns all parts, laid end to end along the dimension named above; each array names one. Nothing has to cross between parts.
Inputs may be any that keep to these rules, and one draw needn't show every extreme that they name: `doc_ids`: document numbers never fall along the sequence and every number appears; each document has 1 to 512 tokens, and one has exactly 512.
All inputs are finite; a program needn't handle non-finite values.
Results may differ from a plain program's by a relative error of at most 0.0054.
Values sent between devices are 32-bit elements; how exact they have to be, the bound alone decides.
No kernel may reach another device: no remote copies, remote signals or barrier semaphores. Data moves between devices by JAX's collectives and lax.ppermute only.
A program may use at most 64 MiB of HBM per device.

v0:
```python
import math

import jax
import jax.numpy as jnp
import numpy as np
from jax import lax
from jax.sharding import PartitionSpec as P

HW = 64
TOK_DEV = 128
FEAT = 2080
MOST = 512


def passed_along(x, axis, by):
    length = lax.axis_size(axis)
    pairs = [(i, i + by) for i in range(length) if 0 <= i + by < length]
    return lax.ppermute(x, axis, pairs)


def pair_tables(breadth):
    first_list = []
    second_list = []
    for column in range(breadth):
        for other in range(column, breadth):
            first_list.append(column)
            second_list.append(other)
    first_idx = np.array(first_list, dtype=np.int32)
    second_idx = np.array(second_list, dtype=np.int32)
    factor_row = np.where(first_idx == second_idx, 1.0, math.sqrt(2.0)).astype(np.float32)
    return (first_idx, second_idx, factor_row)


def selector(breadth):
    first_idx, second_idx, factor_row = pair_tables(breadth)
    lanes = jnp.arange(breadth, dtype=jnp.int32)[:, None]
    pick_first = (lanes == jnp.asarray(first_idx)[None, :]).astype(jnp.bfloat16)
    pick_second = (lanes == jnp.asarray(second_idx)[None, :]).astype(jnp.bfloat16)
    return (jnp.concatenate([pick_first, pick_second], axis=1), jnp.asarray(factor_row))


def expand(rows_in, picker, factor_row):
    feat_count = factor_row.shape[0]
    picked = jnp.dot(rows_in, picker, preferred_element_type=jnp.float32)
    product = picked[:, :feat_count] * picked[:, feat_count:] * factor_row[None, :]
    return product.astype(jnp.bfloat16)


def combine(earlier, later):
    is_empty = later[1][0] < 0.5
    joined = later[0] + jnp.where(
        earlier[1][0] == later[1][0], earlier[0], jnp.zeros_like(earlier[0])
    )
    return (jnp.where(is_empty, earlier[0], joined), jnp.where(is_empty, earlier[1], later[1]))


def per_device(queries, keys, values, doc_ids):
    tok_rows = queries.shape[0]
    head_count = queries.shape[1] // HW
    block_rows = min(512, tok_rows)
    picker, factor_row = selector(HW)
    q_heads = queries.reshape(tok_rows, head_count, HW)
    k_heads = keys.reshape(tok_rows, head_count, HW)
    v_heads = values.reshape(tok_rows, head_count, HW)
    first_id = doc_ids[0]
    last_id = doc_ids[tok_rows - 1]
    masked_v = jnp.where((doc_ids == last_id)[:, None, None], v_heads, jnp.zeros_like(v_heads))
    columns = []
    for head_index in range(head_count):
        state_head = jnp.zeros((FEAT, HW), jnp.float32)
        row_start = 0
        phi_k = expand(k_heads[row_start : row_start + block_rows, head_index], picker, factor_row)
        state_head = state_head + jnp.einsum(
            "tf,tv->fv",
            phi_k,
            masked_v[row_start : row_start + block_rows, head_index],
            preferred_element_type=jnp.float32,
        )
        columns.append(state_head)
    local_state = jnp.concatenate(columns, axis=1)
    last_label = jnp.reshape(last_id + 1, (1,)).astype(jnp.float32)
    target = (first_id + 1).astype(jnp.float32)
    reach_total = MOST // TOK_DEV
    accum = passed_along((local_state, last_label), "ctx", 1)
    span = 1
    while span < reach_total:
        shifted = passed_along((accum[0], accum[1]), "ctx", span)
        accum = combine(shifted, accum)
        span = span * 2
    carried = jnp.where(accum[1][0] == target, accum[0], jnp.zeros_like(accum[0]))
    carried = carried.astype(jnp.bfloat16)
    row_start = 0
    row_stop = row_start + block_rows
    scores = jnp.einsum("thd,shd->hts", q_heads, k_heads, preferred_element_type=jnp.float32)
    row_pos = row_start + jnp.arange(block_rows)[:, None]
    col_pos = jnp.arange(row_stop)[None, :]
    allowed = (row_pos >= col_pos) & (doc_ids[:, None] == doc_ids[None, :row_stop])
    weights = jnp.where(allowed[None], scores * scores, jnp.zeros_like(scores)).astype(jnp.bfloat16)
    intra_part = jnp.einsum("hts,shd->thd", weights, v_heads, preferred_element_type=jnp.float32)
    outputs = []
    for head_index in range(head_count):
        phi_q = expand(q_heads[:, head_index], picker, factor_row)
        outputs.append(
            jnp.dot(
                phi_q,
                carried[:, head_index * HW : (head_index + 1) * HW],
                preferred_element_type=jnp.float32,
            )
        )
    readout = jnp.stack(outputs, axis=1)
    summed = intra_part + jnp.where(
        (doc_ids == first_id)[:, None, None], readout, jnp.zeros_like(readout)
    )
    normed = summed * lax.rsqrt(jnp.mean(summed * summed, axis=-1, keepdims=True) + 1e-06)
    pieces_out = normed.astype(jnp.bfloat16).reshape(block_rows, head_count * HW)
    return pieces_out


def solution(mesh):
    placed = (
        P(("groups", "ctx"), ("heads", "rep")),
        P(("groups", "ctx"), ("heads", "rep")),
        P(("groups", "ctx"), ("heads", "rep")),
        P(("groups", "ctx")),
    )
    return jax.shard_map(
        per_device,
        mesh=mesh,
        in_specs=placed,
        out_specs=P(("groups", "ctx"), ("heads", "rep")),
        check_vma=False,
    )
```

profile of v0, /device:TPU:13, one launch (start us, length us, event | category | flops | bytes accessed | tf_op | source)
XLA Modules:
  0.0 140.3 jit_solution(16289029565216089377)
XLA Ops:
  0.0 0.9 copy.15
  1.0 0.9 iota_compare_fusion
  1.8 2.4 %convolution_bitcast_fusion.6 = f32[128,4160]{0,1:T(8,128)} fusion(bf16[128,4,64]{0,2,1:T(8,128)(2,1)S(1)} %bitcast.80, pred[64,2080]{1,0:T(32,128)(4,1)S(1)} %get-tuple-element.11, pred[64,2080]{1,0:T(32,128)(4,1)S(1)} %get-tuple-element.12), kind=kOutput, calls=%fused_computation.6 | convolution fusion | flops 68423680 | bytes 2424832 | tf_op jit(solution)/shard_map/dot_general | solution.py:44
  4.2 2.3 %convolution_bitcast_fusion.5 = f32[128,4160]{0,1:T(8,128)} fusion(bf16[128,4,64]{0,2,1:T(8,128)(2,1)S(1)} %bitcast.81, pred[64,2080]{1,0:T(32,128)(4,1)S(1)} %get-tuple-element.11, pred[64,2080]{1,0:T(32,128)(4,1)S(1)} %get-tuple-element.12), kind=kOutput, calls=%fused_computation.5 | convolution fusion | flops 68423680 | bytes 2424832 | tf_op jit(solution)/shard_map/dot_general | solution.py:44
  6.6 2.4 %convolution_bitcast_fusion.4 = f32[128,4160]{0,1:T(8,128)} fusion(bf16[128,4,64]{0,2,1:T(8,128)(2,1)S(1)} %bitcast.82, pred[64,2080]{1,0:T(32,128)(4,1)S(1)} %get-tuple-element.11, pred[64,2080]{1,0:T(32,128)(4,1)S(1)} %get-tuple-element.12), kind=kOutput, calls=%fused_computation.4 | convolution fusion | flops 68423680 | bytes 2424832 | tf_op jit(solution)/shard_map/dot_general | solution.py:44
  8.9 1.0 convolution_bitcast_fusion.3
  9.9 0.0 copy-done.9
  9.9 0.7 fusion.49
  10.6 0.1 copy.16
  10.7 0.0 copy-start
  10.7 1.5 %broadcast_compare_fusion.1 = (pred[128]{0:T(512)(128)(4,1)S(1)}, pred[128]{0:T(512)(128)(4,1)S(1)}) fusion(s32[128]{0:T(128)S(1)} %copy-done.9, s32[]{:T(128)} %bitcast.4, s32[]{:T(128)} %bitcast.7), kind=kLoop, calls=%fused_computation.86 | loop fusion | flops 256 | bytes 776 | tf_op jit(solution)/shard_map/eq | solution.py:112
  12.3 2.1 %fusion.22 = f32[2080,64]{0,1:T(8,128)S(1)} fusion(f32[128,4160]{0,1:T(8,128)} %convolution_bitcast_fusion.6, f32[2080]{0:T(1024)S(1)} %copy-done.6, bf16[128,4,64]{0,2,1:T(8,128)(2,1)S(1)} %broadcast_select_fusion), kind=kOutput, calls=%fused_computation.48 | convolution fusion | flops 34877440 | bytes 2691072 | tf_op jit(solution)/shard_map/tf,tv->fv/dot_general | solution.py:73
  14.3 2.1 %fusion.24 = f32[2080,64]{0,1:T(8,128)S(1)} fusion(f32[128,4160]{0,1:T(8,128)} %convolution_bitcast_fusion.5, f32[2080]{0:T(1024)S(1)} %copy-done.6, bf16[128,4,64]{0,2,1:T(8,128)(2,1)S(1)} %broadcast_select_fusion), kind=kOutput, calls=%fused_computation.49 | convolution fusion | flops 34877440 | bytes 2691072 | tf_op jit(solution)/shard_map/tf,tv->fv/dot_general | solution.py:73
  16.4 0.5 fusion.26
  16.9 0.5 fusion.28
  17.4 0.1 pad_maximum_fusion
  17.6 1.9 %copy.17 = f32[2080,256]{1,0:T(8,128)} copy(f32[2080,256]{0,1:T(8,128)S(1)} %pad_maximum_fusion) | data formatting | bytes 4259840 | tf_op jit(solution)/shard_map/concatenate | solution.py:80
  19.5 3.8 %collective-permute-start.3 = (f32[2080,256]{1,0:T(8,128)}, f32[2080,256]{1,0:T(8,128)S(1)}, u32[]{:S(2)}, u32[]{:S(2)}) collective-permute-start(f32[2080,256]{1,0:T(8,128)} %copy.17), channel_id=1, source_target_pairs={{0,2},{2,4},{4,6},{6,8},{8,10},{10,12},{12,14},{1,3},{3,5},{5,7},{... | collective-permute-start | bytes 6389768 | tf_op jit(solution)/shard_map/ppermute | solution.py:18
  23.2 23.6 %collective-permute-done.3 = f32[2080,256]{1,0:T(8,128)S(1)} collective-permute-done((f32[2080,256]{1,0:T(8,128)}, f32[2080,256]{1,0:T(8,128)S(1)}, u32[]{:S(2)}, u32[]{:S(2)}) %collective-permute-start.3) | collective-permute-done | bytes 2129952 | tf_op jit(solution)/shard_map/ppermute | solution.py:18
  46.9 4.3 %collective-permute-start.4 = (f32[2080,256]{1,0:T(8,128)S(1)}, f32[2080,256]{1,0:T(8,128)}, u32[]{:S(2)}, u32[]{:S(2)}) collective-permute-start(f32[2080,256]{1,0:T(8,128)S(1)} %collective-permute-done.3), channel_id=1, source_target_pairs={{0,2},{2,4},{4,6},{6,8},{8,10},{10,12},{12,14},{1,3},{3,5},{5,7},{... | collective-permute-start | bytes 6389768 | tf_op jit(solution)/shard_map/ppermute | solution.py:18
  51.8 22.7 %collective-permute-start = (f32[1]{0:T(128)}, f32[1]{0:T(128)}, u32[]{:S(2)}, u32[]{:S(2)}) collective-permute-start(f32[1]{0:T(128)} %bitcast.8), channel_id=1, source_target_pairs={{0,2},{2,4},{4,6},{6,8},{8,10},{10,12},{12,14},{1,3},{3,5},{5,7},{... | collective-permute-start | bytes 20 | tf_op jit(solution)/shard_map/ppermute | solution.py:18
  74.5 4.5 %collective-permute-start.1 = (f32[1]{0:T(128)}, f32[1]{0:T(128)}, u32[]{:S(2)}, u32[]{:S(2)}) collective-permute-start(f32[1]{0:T(128)} %collective-permute-done), channel_id=1, source_target_pairs={{0,2},{2,4},{4,6},{6,8},{8,10},{10,12},{12,14},{1,3},{3,5},{5,7},{... | collective-permute-start | bytes 20 | tf_op jit(solution)/shard_map/ppermute | solution.py:18
  79.7 0.1 collective-permute-done.1
  80.9 0.0 collective-permute-done.4
  81.0 0.0 copy-done.5
  81.0 0.0 copy-start.8
  81.0 2.5 %add_select_fusion = f32[2080,256]{1,0:T(8,128)S(1)} fusion(f32[2080,256]{1,0:T(8,128)} %collective-permute-done.4, f32[2080,256]{1,0:T(8,128)} %copy-done.5, pred[]{:T(512)} %bitcast.24, pred[]{:T(512)} %bitcast.11), kind=kLoop, calls=%fused_computation.10 | loop fusion | flops 1597440 | bytes 6389762 | tf_op jit(solution)/shard_map/jit(_where)/select_n | solution.py:54
  83.5 3.2 %collective-permute-start.5 = (f32[2080,256]{1,0:T(8,128)S(1)}, f32[2080,256]{1,0:T(8,128)}, u32[]{:S(2)}, u32[]{:S(2)}) collective-permute-start(f32[2080,256]{1,0:T(8,128)S(1)} %add_select_fusion), channel_id=1, source_target_pairs={{0,4},{2,6},{4,8},{6,10},{8,12},{10,14},{1,5},{3,7},{5,9},{7,11},{... | collective-permute-start | bytes 6389768 | tf_op jit(solution)/shard_map/ppermute | solution.py:18
  87.4 0.0 copy-done.8
  87.4 0.1 copy.14
  87.5 0.1 fusion.47
  87.6 2.4 %convolution_bitcast_fusion.2 = f32[128,4160]{0,1:T(8,128)} fusion(bf16[128,4,64]{0,2,1:T(8,128)(2,1)S(1)} %bitcast.85, pred[64,2080]{1,0:T(32,128)(4,1)S(1)} %get-tuple-element.11, pred[64,2080]{1,0:T(32,128)(4,1)S(1)} %get-tuple-element.12), kind=kOutput, calls=%fused_computation.2 | convolution fusion | flops 68423680 | bytes 2424832 | tf_op jit(solution)/shard_map/dot_general | solution.py:44
  90.0 2.4 %convolution_bitcast_fusion.7 = f32[128,4160]{0,1:T(8,128)} fusion(bf16[128,4,64]{0,2,1:T(8,128)(2,1)S(1)} %bitcast.86, pred[64,2080]{1,0:T(32,128)(4,1)S(1)} %get-tuple-element.11, pred[64,2080]{1,0:T(32,128)(4,1)S(1)} %get-tuple-element.12), kind=kOutput, calls=%fused_computation.7 | convolution fusion | flops 68423680 | bytes 2424832 | tf_op jit(solution)/shard_map/dot_general | solution.py:44
  92.4 2.3 %convolution_bitcast_fusion.1 = f32[128,4160]{0,1:T(8,128)} fusion(bf16[128,4,64]{0,2,1:T(8,128)(2,1)S(1)} %bitcast.87, pred[64,2080]{1,0:T(32,128)(4,1)S(1)} %get-tuple-element.11, pred[64,2080]{1,0:T(32,128)(4,1)S(1)} %get-tuple-element.12), kind=kOutput, calls=%fused_computation.1 | convolution fusion | flops 68423680 | bytes 2424832 | tf_op jit(solution)/shard_map/dot_general | solution.py:44
  94.7 2.4 %convolution_bitcast_fusion = f32[128,4160]{0,1:T(8,128)} fusion(bf16[128,4,64]{0,2,1:T(8,128)(2,1)S(1)} %bitcast.88, pred[64,2080]{1,0:T(32,128)(4,1)S(1)} %get-tuple-element.11, pred[64,2080]{1,0:T(32,128)(4,1)S(1)} %get-tuple-element.12), kind=kOutput, calls=%fused_computation | convolution fusion | flops 68423680 | bytes 2424832 | tf_op jit(solution)/shard_map/dot_general | solution.py:44
  98.3 33.0 %collective-permute-start.2 = (f32[1]{0:T(128)}, f32[1]{0:T(128)}, u32[]{:S(2)}, u32[]{:S(2)}) collective-permute-start(f32[1]{0:T(128)} %select_n.55), channel_id=1, source_target_pairs={{0,4},{2,6},{4,8},{6,10},{8,12},{10,14},{1,5},{3,7},{5,9},{7,11},{... | collective-permute-start | bytes 20 | tf_op jit(solution)/shard_map/ppermute | solution.py:18
  131.3 1.0 collective-permute-done.2
  133.3 0.0 collective-permute-done.5
  133.4 2.1 %select_convert_fusion = bf16[2080,256]{1,0:T(8,128)(2,1)S(1)} fusion(f32[2080,256]{1,0:T(8,128)} %collective-permute-done.5, f32[2080,256]{1,0:T(8,128)S(1)} %add_select_fusion, pred[]{:T(512)} %bitcast.25, pred[]{:T(512)} %bitcast.10, pred[]{:T(512)S(6)} %eq.81), kind=kLoop, calls=%fused_computation.9 | loop fusion | flops 2662400 | bytes 5324803 | tf_op jit(solution)/shard_map/convert_element_type | solution.py:91
  135.5 0.1 copy-done.4
  135.6 0.9 convolution_bitcast_fusion.10
  136.5 0.7 convolution_bitcast_fusion.11
  137.2 0.2 copy-done.2
  137.4 0.7 convolution_bitcast_fusion.9
  138.0 0.3 copy-done.1
  138.3 0.9 convolution_bitcast_fusion.8
  139.1 0.4 multiply_reduce_fusion
  139.6 0.7 copy.18
  (16 shorter events, 0.1 us)
Async XLA Ops:
  6.5 3.4 %copy-start.9 = (s32[128]{0:T(128)S(1)}, s32[128]{0:T(128)}, u32[]{:S(2)}) copy-start(s32[128]{0:T(128)} %param.10) | copy-start | bytes 1540
  6.6 4.1 %copy-start.7 = (bf16[128,256]{1,0:T(8,128)(2,1)S(1)}, bf16[128,256]{1,0:T(8,128)(2,1)}, u32[]{:S(2)}) copy-start(bf16[128,256]{1,0:T(8,128)(2,1)} %param.9) | copy-start | bytes 196612
  6.6 5.7 %copy-start.6 = (f32[2080]{0:T(1024)S(1)}, f32[2080]{0:T(1024)}, u32[]{:S(2)}) copy-start(f32[2080]{0:T(1024)} %constant.26.clone) | copy-start | bytes 24964
  10.7 5.7 %copy-start = (f32[128,4160]{0,1:T(8,128)S(1)}, f32[128,4160]{0,1:T(8,128)}, u32[]{:S(2)}) copy-start(f32[128,4160]{0,1:T(8,128)} %convolution_bitcast_fusion.4) | copy-start | bytes 6389764
  19.5 27.4 %collective-permute-start.3 = (f32[2080,256]{1,0:T(8,128)}, f32[2080,256]{1,0:T(8,128)S(1)}, u32[]{:S(2)}, u32[]{:S(2)}) collective-permute-start(f32[2080,256]{1,0:T(8,128)} %copy.17), channel_id=1, source_target_pairs={{0,2},{2,4},{4,6},{6,8},{8,10},{10,12},{12,14},{1,3},{3,5},{5,7},{... | collective-permute-start | bytes 6389768 | tf_op jit(solution)/shard_map/ppermute | solution.py:18
  46.9 34.1 %copy-start.5 = (f32[2080,256]{1,0:T(8,128)}, f32[2080,256]{1,0:T(8,128)S(1)}, u32[]{:S(2)}) copy-start(f32[2080,256]{1,0:T(8,128)S(1)} %collective-permute-done.3) | copy-start | bytes 6389764
  46.9 34.1 %collective-permute-start.4 = (f32[2080,256]{1,0:T(8,128)S(1)}, f32[2080,256]{1,0:T(8,128)}, u32[]{:S(2)}, u32[]{:S(2)}) collective-permute-start(f32[2080,256]{1,0:T(8,128)S(1)} %collective-permute-done.3), channel_id=1, source_target_pairs={{0,2},{2,4},{4,6},{6,8},{8,10},{10,12},{12,14},{1,3},{3,5},{5,7},{... | collective-permute-start | bytes 6389768 | tf_op jit(solution)/shard_map/ppermute | solution.py:18
  51.8 22.7 %collective-permute-start = (f32[1]{0:T(128)}, f32[1]{0:T(128)}, u32[]{:S(2)}, u32[]{:S(2)}) collective-permute-start(f32[1]{0:T(128)} %bitcast.8), channel_id=1, source_target_pairs={{0,2},{2,4},{4,6},{6,8},{8,10},{10,12},{12,14},{1,3},{3,5},{5,7},{... | collective-permute-start | bytes 20 | tf_op jit(solution)/shard_map/ppermute | solution.py:18
  74.5 5.3 %collective-permute-start.1 = (f32[1]{0:T(128)}, f32[1]{0:T(128)}, u32[]{:S(2)}, u32[]{:S(2)}) collective-permute-start(f32[1]{0:T(128)} %collective-permute-done), channel_id=1, source_target_pairs={{0,2},{2,4},{4,6},{6,8},{8,10},{10,12},{12,14},{1,3},{3,5},{5,7},{... | collective-permute-start | bytes 20 | tf_op jit(solution)/shard_map/ppermute | solution.py:18
  81.0 6.4 %copy-start.8 = (bf16[128,256]{1,0:T(8,128)(2,1)S(1)}, bf16[128,256]{1,0:T(8,128)(2,1)}, u32[]{:S(2)}) copy-start(bf16[128,256]{1,0:T(8,128)(2,1)} %param.7) | copy-start | bytes 196612
  83.5 49.8 %collective-permute-start.5 = (f32[2080,256]{1,0:T(8,128)S(1)}, f32[2080,256]{1,0:T(8,128)}, u32[]{:S(2)}, u32[]{:S(2)}) collective-permute-start(f32[2080,256]{1,0:T(8,128)S(1)} %add_select_fusion), channel_id=1, source_target_pairs={{0,4},{2,6},{4,8},{6,10},{8,12},{10,14},{1,5},{3,7},{5,9},{7,11},{... | collective-permute-start | bytes 6389768 | tf_op jit(solution)/shard_map/ppermute | solution.py:18
  98.3 34.0 %collective-permute-start.2 = (f32[1]{0:T(128)}, f32[1]{0:T(128)}, u32[]{:S(2)}, u32[]{:S(2)}) collective-permute-start(f32[1]{0:T(128)} %select_n.55), channel_id=1, source_target_pairs={{0,4},{2,6},{4,8},{6,10},{8,12},{10,14},{1,5},{3,7},{5,9},{7,11},{... | collective-permute-start | bytes 20 | tf_op jit(solution)/shard_map/ppermute | solution.py:18
  133.4 2.2 %copy-start.4 = (f32[128,4160]{0,1:T(8,128)S(1)}, f32[128,4160]{0,1:T(8,128)}, u32[]{:S(2)}) copy-start(f32[128,4160]{0,1:T(8,128)} %convolution_bitcast_fusion.2) | copy-start | bytes 6389764
  133.4 3.1 %copy-start.3 = (f32[128,4160]{0,1:T(8,128)S(1)}, f32[128,4160]{0,1:T(8,128)}, u32[]{:S(2)}) copy-start(f32[128,4160]{0,1:T(8,128)} %convolution_bitcast_fusion.7) | copy-start | bytes 6389764
  135.6 1.8 %copy-start.2 = (f32[128,4160]{0,1:T(8,128)S(1)}, f32[128,4160]{0,1:T(8,128)}, u32[]{:S(2)}) copy-start(f32[128,4160]{0,1:T(8,128)} %convolution_bitcast_fusion.1) | copy-start | bytes 6389764
  136.5 1.8 %copy-start.1 = (f32[128,4160]{0,1:T(8,128)S(1)}, f32[128,4160]{0,1:T(8,128)}, u32[]{:S(2)}) copy-start(f32[128,4160]{0,1:T(8,128)} %convolution_bitcast_fusion) | copy-start | bytes 6389764
where the time goes:
time: 143 us; the launch traced here: 140 us
  starting transfers between devices  71.4 us (50%)
  matrix products  26.2 us (18%)
  waiting for transfers between devices  24.7 us (17%)
  other arithmetic  7.28 us (5%)
  between operations  5.65 us (4%)
  local copies, waits for them, and re-layouts  5.06 us (4%)
    ppermute x6, starting transfers between devices, passed_along(): return lax.ppermute(x, axis, pairs)  71.4 us
    ppermute x6, waiting for transfers between devices, passed_along(): return lax.ppermute(x, axis, pairs)  24.7 us
    dot_general x8, matrix products, expand(): picked = jnp.dot(rows_in, picker, preferred_element_type=jnp.float32)  17.6 us
    dot_general x4, matrix products, per_device(): jnp.einsum('tf,tv->fv', phi_k, masked_v[row_start:row_start + block_rows,...  5.17 us
    dot_general x4, matrix products, per_device(): jnp.dot(phi_q, carried[:, head_index * HW:(head_index + 1) * HW], preferr...  3.07 us
  transfers between devices with their start and end apart: 6, of which 3 were waited for; matrix products, arithmetic and copies ran while one was open for 7% of the time, Pallas kernels for 0%

commit v1 on v0

v1 whole, which is shorter than its diff:
```python
import functools

import jax
import jax.numpy as jnp
from jax import lax
from jax.experimental import pallas as pl
from jax.experimental.pallas import tpu as pltpu
from jax.sharding import PartitionSpec as P

HW = 64
MOST = 512
LANES = 128
TILE = 8
EPS = 1e-06
GRANT = 16 << 20


def chip_moves(length, first):
    couples = length // 2
    cycle = couples - first
    pairs = []
    for couple in range(couples):
        for side in range(2):
            if couple < first or cycle < 2:
                pairs.append((2 * couple + side, 2 * couple + 1 - side))
            else:
                target = couple + 1 if couple + 1 < couples else first
                pairs.append((2 * couple + side, 2 * target + side))
    return pairs


def trade(x):
    length = lax.axis_size("ctx")
    return lax.ppermute(x, "ctx", [(i, i ^ 1) for i in range(length)])


def lower_half(shape):
    return lax.broadcasted_iota(jnp.int32, shape, 1) % LANES < HW


def two_heads(block):
    low = lower_half(block.shape)
    zero = jnp.zeros_like(block)
    both = jnp.concatenate([jnp.where(low, block, zero), jnp.where(low, zero, block)], axis=0)
    return both.astype(jnp.bfloat16)


def attend(q_two, k_block, v_block, mask):
    scores = lax.dot_general(
        q_two, two_heads(k_block), (((1,), (1,)), ((), ())), preferred_element_type=jnp.float32
    )
    weights = jnp.where(mask, scores * scores, jnp.zeros_like(scores)).astype(jnp.bfloat16)
    return jnp.dot(weights, two_heads(v_block), preferred_element_type=jnp.float32)


def head_pair(ref, pair, rows):
    return ref[pair * rows : (pair + 1) * rows, :]


def pack_body(k_ref, v_ref, ids_ref, kp_ref, vp_ref):
    rows = k_ref.shape[0]
    for pair in range(k_ref.shape[1] // LANES):
        cut = slice(pair * LANES, (pair + 1) * LANES)
        kp_ref[pair * rows : (pair + 1) * rows, :] = k_ref[:, cut].astype(jnp.float32)
        vp_ref[pair * rows : (pair + 1) * rows, :] = v_ref[:, cut].astype(jnp.float32)
    ids = ids_ref[...].astype(jnp.float32)
    kp_ref[kp_ref.shape[0] - TILE :, :] = jnp.broadcast_to(ids, (TILE, rows))


def earlier_blocks(q_ref, ids_ref, blocks):
    rows = q_ref.shape[0]
    ids = ids_ref[...].astype(jnp.float32)
    first = ids[:, 0:1]
    count = jnp.sum(jnp.where(ids == first, 1.0, 0.0), axis=1, keepdims=True)
    seen = lax.broadcasted_iota(jnp.int32, (rows, LANES), 0).astype(jnp.float32) < count
    parts = []
    for pair in range(q_ref.shape[1] // LANES):
        q_two = q_ref[:, pair * LANES : (pair + 1) * LANES]
        total = jnp.zeros((rows, LANES), jnp.float32)
        for k_ref, v_ref, usable in blocks:
            top = k_ref.shape[0] - TILE
            there = k_ref[top : top + 1, :]
            mask = jnp.where(usable, there, -1.0) == first
            mask = jnp.concatenate([mask, mask], axis=1)
            total = total + attend(
                q_two, head_pair(k_ref, pair, rows), head_pair(v_ref, pair, rows), mask
            )
        parts.append(jnp.where(seen, total, jnp.zeros_like(total)))
    return parts


def local_body(q_ref, k_ref, v_ref, ids_ref, sk_ref, sv_ref, y_ref):
    rows = q_ref.shape[0]
    odd = lax.axis_index("ctx") % 2 == 1
    ids = ids_ref[...].astype(jnp.float32)
    row_pos = lax.broadcasted_iota(jnp.int32, (rows, rows), 0)
    col_pos = lax.broadcasted_iota(jnp.int32, (rows, rows), 1)
    tall = jnp.sum(jnp.where(row_pos == col_pos, ids, 0.0), axis=1, keepdims=True)
    allowed = (row_pos >= col_pos) & (tall == ids)
    allowed = jnp.concatenate([allowed, allowed], axis=1)
    far = earlier_blocks(q_ref, ids_ref, [(sk_ref, sv_ref, odd)])
    for pair in range(q_ref.shape[1] // LANES):
        cut = slice(pair * LANES, (pair + 1) * LANES)
        near = attend(
            q_ref[:, cut],
            k_ref[:, cut].astype(jnp.float32),
            v_ref[:, cut].astype(jnp.float32),
            allowed,
        )
        y_ref[pair * rows : (pair + 1) * rows, :] = near + far[pair]


def add_body(back, q_ref, ids_ref, y_ref, k_ref, v_ref, sk_ref, sv_ref, o_ref):
    rows = q_ref.shape[0]
    usable = lax.axis_index("ctx") >= 2 * back
    far = earlier_blocks(q_ref, ids_ref, [(k_ref, v_ref, usable), (sk_ref, sv_ref, usable)])
    for pair in range(q_ref.shape[1] // LANES):
        o_ref[pair * rows : (pair + 1) * rows, :] = head_pair(y_ref, pair, rows) + far[pair]


def last_body(back, q_ref, ids_ref, y_ref, k_ref, v_ref, sk_ref, sv_ref, o_ref):
    rows = q_ref.shape[0]
    usable = lax.axis_index("ctx") >= 2 * back
    far = earlier_blocks(q_ref, ids_ref, [(k_ref, v_ref, usable), (sk_ref, sv_ref, usable)])
    low = lower_half((rows, LANES))
    for pair in range(q_ref.shape[1] // LANES):
        y = head_pair(y_ref, pair, rows) + far[pair]
        square = y * y
        sum_low = jnp.sum(jnp.where(low, square, 0.0), axis=1, keepdims=True)
        sum_high = jnp.sum(jnp.where(low, 0.0, square), axis=1, keepdims=True)
        mean = jnp.where(low, sum_low, sum_high) * (1.0 / HW)
        o_ref[:, pair * LANES : (pair + 1) * LANES] = (y * lax.rsqrt(mean + EPS)).astype(o_ref.dtype)


def call(body, out, name, flops, *args):
    moved = sum(a.size * a.dtype.itemsize for a in args)
    return pl.pallas_call(
        body,
        out_shape=out,
        name=name,
        cost_estimate=pl.CostEstimate(flops=flops, bytes_accessed=moved, transcendentals=0),
        compiler_params=pltpu.CompilerParams(vmem_limit_bytes=GRANT),
    )(*args)


def per_device(queries, keys, values, doc_ids):
    rows, columns = queries.shape
    assert columns % LANES == 0 and rows == LANES
    length = lax.axis_size("ctx")
    assert length % 2 == 0
    reach = -(-MOST // rows)
    hops = -(-reach // 2)
    pairs = columns // LANES
    flat = pairs * rows
    one = 4 * rows * rows * columns
    ids = doc_ids.reshape(1, rows)
    y_shape = jax.ShapeDtypeStruct((flat, LANES), jnp.float32)
    packed = (jax.ShapeDtypeStruct((flat + TILE, LANES), jnp.float32), y_shape)
    k_now, v_now = call(pack_body, packed, "pack", 0, keys, values, ids)
    k_side, v_side = trade(k_now), trade(v_now)
    y = call(local_body, y_shape, "local", 2 * one, queries, keys, values, ids, k_side, v_side)
    for back in range(1, hops + 1):
        moves = chip_moves(length, back - 1)
        k_now, v_now = lax.ppermute(k_now, "ctx", moves), lax.ppermute(v_now, "ctx", moves)
        k_side, v_side = trade(k_now), trade(v_now)
        last = back == hops
        body = functools.partial(last_body if last else add_body, back)
        out = jax.ShapeDtypeStruct((rows, columns), jnp.bfloat16) if last else y_shape
        y = call(body, out, f"far{back}", 2 * one, queries, ids, y, k_now, v_now, k_side, v_side)
    return y


def solution(mesh):
    placed = P(("groups", "ctx"), ("heads", "rep"))
    return jax.shard_map(
        per_device,
        mesh=mesh,
        in_specs=(placed, placed, placed, P(("groups", "ctx"))),
        out_specs=placed,
        check_vma=False,
    )
```

time: 143 us -> 20.8 us (0.15); the launches traced: 140 us -> 20.6 us
  starting transfers between devices: 71.4 us -> 13 us
  matrix products: 26.2 us -> 0 us
  waiting for transfers between devices: 24.7 us -> 2.95 us
  other arithmetic: 7.28 us -> 0 us
  between operations: 5.65 us -> 0.06 us
  local copies, waits for them, and re-layouts: 5.06 us -> 2.34 us
  Pallas kernels: 0 us -> 2.28 us
    ppermute x6 -> x10, starting transfers between devices: 71.4 us -> 13 us  [the longest x6 7.72 us: trade(): return lax.ppermute(x, 'ctx', [(i, i ^ 1) for i in range(length)])]
    dot_general x17 -> x0, matrix products: 26.2 us -> none  [the longest x8 17.6 us: expand(): picked = jnp.dot(rows_in, picker, preferred_element_type=jnp.float32)]
    ppermute x6 -> x10, waiting for transfers between devices: 24.7 us -> 2.95 us  [the longest x2 1.88 us: per_device(): lax.ppermute(k_now, 'ctx', moves)]
    select_n x2 -> x0, other arithmetic: 2.56 us -> none  [the longest x1 2.55 us: combine(): jnp.where(is_empty, earlier[0], joined)]
    eq x2 -> x0, other arithmetic: 2.38 us -> none  [the longest x1 1.49 us: per_device(): doc_ids == first_id]
    pallas_call x0 -> x4, Pallas kernels: none -> 2.28 us  [call(): pl.pallas_call(body, out_shape=out, name=name, cost_estimate=pl.CostEstim...]
    convert_element_type x2 -> x0, other arithmetic: 2.1 us -> none  [the longest x1 2.07 us: per_device(): carried = carried.astype(jnp.bfloat16)]
    concatenate x1 -> x0, local copies, waits for them, and re-layouts: 1.87 us -> none  [per_device(): local_state = jnp.concatenate(columns, axis=1)]
  transfers between devices with their start and end apart: 6 -> 10, of which waited for: 3 -> 2; matrix products, arithmetic and copies ran while one was open for 7% -> 0% of each run, Pallas kernels for 0% -> 5%
where the time goes in v1:
time: 20.8 us; the launch traced here: 20.6 us
  starting transfers between devices  13 us (62%)
  waiting for transfers between devices  2.95 us (14%)
  local copies, waits for them, and re-layouts  2.34 us (11%)
  Pallas kernels  2.28 us (11%)
    ppermute x6, starting transfers between devices, trade(): return lax.ppermute(x, 'ctx', [(i, i ^ 1) for i in range(length)])  7.72 us
    ppermute x2, starting transfers between devices, per_device(): lax.ppermute(k_now, 'ctx', moves)  2.65 us
    ppermute x2, starting transfers between devices, per_device(): lax.ppermute(v_now, 'ctx', moves)  2.59 us
    unnamed x8, local copies, waits for them, and re-layouts  2.34 us
    pallas_call x4, Pallas kernels, call(): pl.pallas_call(body, out_shape=out, name=name, cost_estimate=pl.CostEstim...  2.28 us
    ppermute x2, waiting for transfers between devices, per_device(): lax.ppermute(k_now, 'ctx', moves)  1.88 us
    ppermute x2, waiting for transfers between devices, per_device(): lax.ppermute(v_now, 'ctx', moves)  1.05 us
  transfers between devices with their start and end apart: 10, of which 2 were waited for; matrix products, arithmetic and copies ran while one was open for 0% of the time, Pallas kernels for 5%

profile of v1, /device:TPU:13, one launch (start us, length us, event | category | flops | bytes accessed | tf_op | source)
XLA Modules:
  0.0 20.6 jit_solution(432899554826988195)
XLA Ops:
  0.0 0.0 copy-start.3
  0.0 0.7 %copy-done.3 = s32[128]{0:T(128)S(1)} copy-done((s32[128]{0:T(128)S(1)}, s32[128]{0:T(128)}, u32[]{:S(2)}) %copy-start.3) | copy-done | bytes 536
  0.7 0.0 copy-start.1
  0.7 0.8 %copy-done.1 = bf16[128,256]{1,0:T(8,128)(2,1)S(1)} copy-done((bf16[128,256]{1,0:T(8,128)(2,1)S(1)}, bf16[128,256]{1,0:T(8,128)(2,1)}, u32[]{:S(2)}) %copy-start.1) | copy-done | bytes 65560
  1.5 0.0 copy-start.2
  1.5 0.8 %copy-done.2 = bf16[128,256]{1,0:T(8,128)(2,1)S(1)} copy-done((bf16[128,256]{1,0:T(8,128)(2,1)S(1)}, bf16[128,256]{1,0:T(8,128)(2,1)}, u32[]{:S(2)}) %copy-start.2) | copy-done | bytes 65560
  2.3 0.0 copy-start
  2.4 1.3 %collective-permute-start.2 = (f32[264,128]{1,0:T(8,128)S(1)}, f32[264,128]{1,0:T(8,128)S(1)}, u32[]{:S(2)}, u32[]{:S(2)}) collective-permute-start(f32[264,128]{1,0:T(8,128)S(1)} %get-tuple-element.7), channel_id=1, source_target_pairs={{0,4},{2,6},{4,8},{6,10},{8,12},{10,14},{12,0},{14,2},{1,5},{3,7},... | collective-permute-start | bytes 405512 | tf_op jit(solution)/shard_map/ppermute | solution.py:164
  3.7 1.3 %collective-permute-start.3 = (f32[256,128]{1,0:T(8,128)S(1)}, f32[256,128]{1,0:T(8,128)S(1)}, u32[]{:S(2)}, u32[]{:S(2)}) collective-permute-start(f32[256,128]{1,0:T(8,128)S(1)} %get-tuple-element.8), channel_id=1, source_target_pairs={{0,4},{2,6},{4,8},{6,10},{8,12},{10,14},{12,0},{14,2},{1,5},{3,7},... | collective-permute-start | bytes 393224 | tf_op jit(solution)/shard_map/ppermute | solution.py:164
  5.0 1.9 %collective-permute-done.2.k_ref = f32[264,128]{1,0:T(8,128)S(1)} collective-permute-done((f32[264,128]{1,0:T(8,128)S(1)}, f32[264,128]{1,0:T(8,128)S(1)}, u32[]{:S(2)}, u32[]{:S(2)}) %collective-permute-start.2) | collective-permute-done | bytes 135200 | tf_op jit(solution)/shard_map/ppermute | solution.py:164
  6.9 1.3 %collective-permute-start.6 = (f32[264,128]{1,0:T(8,128)S(1)}, f32[264,128]{1,0:T(8,128)S(1)}, u32[]{:S(2)}, u32[]{:S(2)}) collective-permute-start(f32[264,128]{1,0:T(8,128)S(1)} %collective-permute-done.2.k_ref), channel_id=1, source_target_pairs={{0,2},{2,0},{4,8},{6,10},{8,12},{10,14},{12,4},{14,6},{1,3},{3,1},... | collective-permute-start | bytes 405512 | tf_op jit(solution)/shard_map/ppermute | solution.py:164
  8.2 2.9 %collective-permute-start.1 = (f32[256,128]{1,0:T(8,128)S(1)}, f32[256,128]{1,0:T(8,128)S(1)}, u32[]{:S(2)}, u32[]{:S(2)}) collective-permute-start(f32[256,128]{1,0:T(8,128)S(1)} %get-tuple-element.8), channel_id=1, source_target_pairs={{0,2},{2,0},{4,6},{6,4},{8,10},{10,8},{12,14},{14,12},{1,3},{3,1},... | collective-permute-start | bytes 393224 | tf_op jit(solution)/shard_map/ppermute | solution.py:34
  11.1 0.0 collective-permute-done.3.v_ref
  11.1 1.3 %collective-permute-start.7 = (f32[256,128]{1,0:T(8,128)S(1)}, f32[256,128]{1,0:T(8,128)S(1)}, u32[]{:S(2)}, u32[]{:S(2)}) collective-permute-start(f32[256,128]{1,0:T(8,128)S(1)} %collective-permute-done.3.v_ref), channel_id=1, source_target_pairs={{0,2},{2,0},{4,8},{6,10},{8,12},{10,14},{12,4},{14,6},{1,3},{3,1},... | collective-permute-start | bytes 393224 | tf_op jit(solution)/shard_map/ppermute | solution.py:164
  12.4 1.5 %collective-permute-start = (f32[264,128]{1,0:T(8,128)S(1)}, f32[264,128]{1,0:T(8,128)S(1)}, u32[]{:S(2)}, u32[]{:S(2)}) collective-permute-start(f32[264,128]{1,0:T(8,128)S(1)} %get-tuple-element.7), channel_id=1, source_target_pairs={{0,2},{2,0},{4,6},{6,4},{8,10},{10,8},{12,14},{14,12},{1,3},{3,1},... | collective-permute-start | bytes 405512 | tf_op jit(solution)/shard_map/ppermute | solution.py:34
  13.9 0.0 collective-permute-start.4
  13.9 0.0 collective-permute-done.6.k_ref
  13.9 1.8 %collective-permute-start.8 = (f32[264,128]{1,0:T(8,128)S(1)}, f32[264,128]{1,0:T(8,128)S(1)}, u32[]{:S(2)}, u32[]{:S(2)}) collective-permute-start(f32[264,128]{1,0:T(8,128)S(1)} %collective-permute-done.6.k_ref), channel_id=1, source_target_pairs={{0,2},{2,0},{4,6},{6,4},{8,10},{10,8},{12,14},{14,12},{1,3},{3,1},... | collective-permute-start | bytes 405512 | tf_op jit(solution)/shard_map/ppermute | solution.py:34
  15.8 0.0 collective-permute-done.1.sv_ref
  15.8 0.0 collective-permute-start.5
  15.8 1.1 %collective-permute-done.7.v_ref = f32[256,128]{1,0:T(8,128)S(1)} collective-permute-done((f32[256,128]{1,0:T(8,128)S(1)}, f32[256,128]{1,0:T(8,128)S(1)}, u32[]{:S(2)}, u32[]{:S(2)}) %collective-permute-start.7) | collective-permute-done | bytes 131104 | tf_op jit(solution)/shard_map/ppermute | solution.py:164
  16.8 1.4 %collective-permute-start.9 = (f32[256,128]{1,0:T(8,128)S(1)}, f32[256,128]{1,0:T(8,128)S(1)}, u32[]{:S(2)}, u32[]{:S(2)}) collective-permute-start(f32[256,128]{1,0:T(8,128)S(1)} %collective-permute-done.7.v_ref), channel_id=1, source_target_pairs={{0,2},{2,0},{4,6},{6,4},{8,10},{10,8},{12,14},{14,12},{1,3},{3,1},... | collective-permute-start | bytes 393224 | tf_op jit(solution)/shard_map/ppermute | solution.py:34
  18.3 0.0 collective-permute-done.sk_ref
  18.3 0.0 copy-done
  18.3 0.5 %local.1.y_ref = f32[256,128]{1,0:T(8,128)S(1)} custom-call(bf16[128,256]{1,0:T(8,128)(2,1)S(1)} %copy-done, bf16[128,256]{1,0:T(8,128)(2,1)S(1)} %copy-done.1, bf16[128,256]{1,0:T(8,128)(2,1)S(1)} %copy-done.2, s32[1,128]{1,0:T(1,128)S(1)} %bitcast.2, f32[264,128]{1,0:T(8,128)S(1)} %collective-permute-done.sk_ref, f32[256,128]{1,0:T(8,128)S(1)} %collective-permute-done.1.sv_ref), custom_call_target="tpu_custom_call" | custom-call | flops 33554432 | bytes 463360 | tf_op jit(solution)/shard_map/local/pallas_call | solution.py:137
  18.8 0.0 collective-permute-done.5.sv_ref
  18.8 0.0 collective-permute-done.4.sk_ref
  18.8 0.5 %far1.1.y_ref = f32[256,128]{1,0:T(8,128)S(1)} custom-call(bf16[128,256]{1,0:T(8,128)(2,1)S(1)} %copy-done, s32[1,128]{1,0:T(1,128)S(1)} %bitcast.3, f32[256,128]{1,0:T(8,128)S(1)} %local.1.y_ref, f32[264,128]{1,0:T(8,128)S(1)} %collective-permute-done.2.k_ref, f32[256,128]{1,0:T(8,128)S(1)} %collective-permute-done.3.v_ref, ...), custom_call_target="tpu_custom_call" | custom-call | flops 33554432 | bytes 729600 | tf_op jit(solution)/shard_map/far1/pallas_call | solution.py:137
  19.3 0.0 collective-permute-done.9.sv_ref
  19.3 0.0 collective-permute-done.8.sk_ref
  19.4 1.2 %far2.1 = bf16[128,256]{1,0:T(8,128)(2,1)} custom-call(bf16[128,256]{1,0:T(8,128)(2,1)S(1)} %copy-done, s32[1,128]{1,0:T(1,128)S(1)} %bitcast.4, f32[256,128]{1,0:T(8,128)S(1)} %far1.1.y_ref, f32[264,128]{1,0:T(8,128)S(1)} %collective-permute-done.6.k_ref, f32[256,128]{1,0:T(8,128)S(1)} %collective-permute-done.7.v_ref, ...), custom_call_target="tpu_custom_call" | custom-call | flops 33554432 | bytes 729600 | tf_op jit(solution)/shard_map/far2/pallas_call | solution.py:137
  (1 shorter events, 0.0 us)
Async XLA Ops:
  0.0 0.7 %copy-start.3 = (s32[128]{0:T(128)S(1)}, s32[128]{0:T(128)}, u32[]{:S(2)}) copy-start(s32[128]{0:T(128)} %param.7) | copy-start | bytes 1540
  0.7 0.8 %copy-start.1 = (bf16[128,256]{1,0:T(8,128)(2,1)S(1)}, bf16[128,256]{1,0:T(8,128)(2,1)}, u32[]{:S(2)}) copy-start(bf16[128,256]{1,0:T(8,128)(2,1)} %k_ref.3) | copy-start | bytes 196612
  1.5 0.8 %copy-start.2 = (bf16[128,256]{1,0:T(8,128)(2,1)S(1)}, bf16[128,256]{1,0:T(8,128)(2,1)}, u32[]{:S(2)}) copy-start(bf16[128,256]{1,0:T(8,128)(2,1)} %v_ref.3) | copy-start | bytes 196612
  2.3 15.9 %copy-start = (bf16[128,256]{1,0:T(8,128)(2,1)S(1)}, bf16[128,256]{1,0:T(8,128)(2,1)}, u32[]{:S(2)}) copy-start(bf16[128,256]{1,0:T(8,128)(2,1)} %q_ref.5) | copy-start | bytes 196612
  2.4 4.5 %collective-permute-start.2 = (f32[264,128]{1,0:T(8,128)S(1)}, f32[264,128]{1,0:T(8,128)S(1)}, u32[]{:S(2)}, u32[]{:S(2)}) collective-permute-start(f32[264,128]{1,0:T(8,128)S(1)} %get-tuple-element.7), channel_id=1, source_target_pairs={{0,4},{2,6},{4,8},{6,10},{8,12},{10,14},{12,0},{14,2},{1,5},{3,7},... | collective-permute-start | bytes 405512 | tf_op jit(solution)/shard_map/ppermute | solution.py:164
  3.7 7.4 %collective-permute-start.3 = (f32[256,128]{1,0:T(8,128)S(1)}, f32[256,128]{1,0:T(8,128)S(1)}, u32[]{:S(2)}, u32[]{:S(2)}) collective-permute-start(f32[256,128]{1,0:T(8,128)S(1)} %get-tuple-element.8), channel_id=1, source_target_pairs={{0,4},{2,6},{4,8},{6,10},{8,12},{10,14},{12,0},{14,2},{1,5},{3,7},... | collective-permute-start | bytes 393224 | tf_op jit(solution)/shard_map/ppermute | solution.py:164
  6.9 7.1 %collective-permute-start.6 = (f32[264,128]{1,0:T(8,128)S(1)}, f32[264,128]{1,0:T(8,128)S(1)}, u32[]{:S(2)}, u32[]{:S(2)}) collective-permute-start(f32[264,128]{1,0:T(8,128)S(1)} %collective-permute-done.2.k_ref), channel_id=1, source_target_pairs={{0,2},{2,0},{4,8},{6,10},{8,12},{10,14},{12,4},{14,6},{1,3},{3,1},... | collective-permute-start | bytes 405512 | tf_op jit(solution)/shard_map/ppermute | solution.py:164
  8.2 7.6 %collective-permute-start.1 = (f32[256,128]{1,0:T(8,128)S(1)}, f32[256,128]{1,0:T(8,128)S(1)}, u32[]{:S(2)}, u32[]{:S(2)}) collective-permute-start(f32[256,128]{1,0:T(8,128)S(1)} %get-tuple-element.8), channel_id=1, source_target_pairs={{0,2},{2,0},{4,6},{6,4},{8,10},{10,8},{12,14},{14,12},{1,3},{3,1},... | collective-permute-start | bytes 393224 | tf_op jit(solution)/shard_map/ppermute | solution.py:34
  11.1 5.7 %collective-permute-start.7 = (f32[256,128]{1,0:T(8,128)S(1)}, f32[256,128]{1,0:T(8,128)S(1)}, u32[]{:S(2)}, u32[]{:S(2)}) collective-permute-start(f32[256,128]{1,0:T(8,128)S(1)} %collective-permute-done.3.v_ref), channel_id=1, source_target_pairs={{0,2},{2,0},{4,8},{6,10},{8,12},{10,14},{12,4},{14,6},{1,3},{3,1},... | collective-permute-start | bytes 393224 | tf_op jit(solution)/shard_map/ppermute | solution.py:164
  12.4 5.8 %collective-permute-start = (f32[264,128]{1,0:T(8,128)S(1)}, f32[264,128]{1,0:T(8,128)S(1)}, u32[]{:S(2)}, u32[]{:S(2)}) collective-permute-start(f32[264,128]{1,0:T(8,128)S(1)} %get-tuple-element.7), channel_id=1, source_target_pairs={{0,2},{2,0},{4,6},{6,4},{8,10},{10,8},{12,14},{14,12},{1,3},{3,1},... | collective-permute-start | bytes 405512 | tf_op jit(solution)/shard_map/ppermute | solution.py:34
  13.9 4.9 %collective-permute-start.4 = (f32[264,128]{1,0:T(8,128)S(1)}, f32[264,128]{1,0:T(8,128)S(1)}, u32[]{:S(2)}, u32[]{:S(2)}) collective-permute-start(f32[264,128]{1,0:T(8,128)S(1)} %collective-permute-done.2.k_ref), channel_id=1, source_target_pairs={{0,2},{2,0},{4,6},{6,4},{8,10},{10,8},{12,14},{14,12},{1,3},{3,1},... | collective-permute-start | bytes 405512 | tf_op jit(solution)/shard_map/ppermute | solution.py:34
  13.9 5.4 %collective-permute-start.8 = (f32[264,128]{1,0:T(8,128)S(1)}, f32[264,128]{1,0:T(8,128)S(1)}, u32[]{:S(2)}, u32[]{:S(2)}) collective-permute-start(f32[264,128]{1,0:T(8,128)S(1)} %collective-permute-done.6.k_ref), channel_id=1, source_target_pairs={{0,2},{2,0},{4,6},{6,4},{8,10},{10,8},{12,14},{14,12},{1,3},{3,1},... | collective-permute-start | bytes 405512 | tf_op jit(solution)/shard_map/ppermute | solution.py:34
  15.8 3.0 %collective-permute-start.5 = (f32[256,128]{1,0:T(8,128)S(1)}, f32[256,128]{1,0:T(8,128)S(1)}, u32[]{:S(2)}, u32[]{:S(2)}) collective-permute-start(f32[256,128]{1,0:T(8,128)S(1)} %collective-permute-done.3.v_ref), channel_id=1, source_target_pairs={{0,2},{2,0},{4,6},{6,4},{8,10},{10,8},{12,14},{14,12},{1,3},{3,1},... | collective-permute-start | bytes 393224 | tf_op jit(solution)/shard_map/ppermute | solution.py:34
  16.8 2.5 %collective-permute-start.9 = (f32[256,128]{1,0:T(8,128)S(1)}, f32[256,128]{1,0:T(8,128)S(1)}, u32[]{:S(2)}, u32[]{:S(2)}) collective-permute-start(f32[256,128]{1,0:T(8,128)S(1)} %collective-permute-done.7.v_ref), channel_id=1, source_target_pairs={{0,2},{2,0},{4,6},{6,4},{8,10},{10,8},{12,14},{14,12},{1,3},{3,1},... | collective-permute-start | bytes 393224 | tf_op jit(solution)/shard_map/ppermute | solution.py:34

commit v2 on v1

v2 whole, which is shorter than its diff:
```python
import functools

import jax
import jax.numpy as jnp
from jax import lax
from jax.experimental import pallas as pl
from jax.experimental.pallas import tpu as pltpu
from jax.sharding import PartitionSpec as P


HW = 64
MOST = 512
LANES = 128
TILE = 8
EPS = 1e-06
GRANT = 16 << 20


def snake(x, rising, first):
    couples = lax.axis_size("ctx") // 2
    pairs = []
    for couple in range(couples):
        up, down = 2 * couple + rising, 2 * couple + 1 - rising
        pairs.append((up, up + 2 if first <= couple < couples - 1 else down))
        pairs.append((down, down - 2 if couple > first else up))
    return lax.ppermute(x, "ctx", pairs)


def climb(x, first):
    couples = lax.axis_size("ctx") // 2
    pairs = []
    for couple in range(couples):
        for side in range(2):
            here, stay = 2 * couple + side, couple < first or couples - first < 2
            target = couple + 1 if couple + 1 < couples else first
            pairs.append((here, here ^ 1 if stay else 2 * target + side))
    return lax.ppermute(x, "ctx", pairs)


def rise(x, first):
    length = lax.axis_size("ctx")
    return lax.ppermute(x, "ctx", [(i, i + 2) for i in range(2 * first, length - 2)])


def trade(x):
    return lax.ppermute(x, "ctx", [(i, i ^ 1) for i in range(lax.axis_size("ctx"))])


def is_odd():
    return lax.axis_index("ctx") % 2 == 1


def lower_half(shape):
    return lax.broadcasted_iota(jnp.int32, shape, 1) % LANES < HW


def two_heads(block):
    low = lower_half(block.shape)
    zero = jnp.zeros_like(block)
    both = jnp.concatenate([jnp.where(low, block, zero), jnp.where(low, zero, block)], axis=0)
    return both.astype(jnp.bfloat16)


def attend(q_two, keys, values, mask):
    scores = lax.dot_general(
        q_two, two_heads(keys), (((1,), (1,)), ((), ())), preferred_element_type=jnp.float32
    )
    mask = jnp.concatenate([mask, mask], axis=1)
    weights = jnp.where(mask, scores * scores, jnp.zeros_like(scores)).astype(jnp.bfloat16)
    return jnp.dot(weights, two_heads(values), preferred_element_type=jnp.float32)


def pick(flag, this, other, start, size):
    return jnp.where(flag, this[start : start + size, :], other[start : start + size, :])


def pick_ids(flag, this, other):
    return pick(flag, this, other, this.shape[0] - TILE, 1)


def pick_pair(flag, these, others, pair, rows):
    this, other = these[pair], others[pair]
    return pick(flag, this, other, 0, rows), pick(flag, this, other, rows, rows)


def rows_of_first(ids):
    count = jnp.sum(jnp.where(ids == ids[:, 0:1], 1.0, 0.0), axis=1, keepdims=True)
    shape = (ids.shape[1], LANES)
    return lax.broadcasted_iota(jnp.int32, shape, 0).astype(jnp.float32) < count


def cut(pair):
    return slice(pair * LANES, (pair + 1) * LANES)


def groups_of(refs, count, pairs):
    return [refs[at * pairs : (at + 1) * pairs] for at in range(count)], refs[count * pairs :]


def pack_body(pairs, k_hbm, v_hbm, q_hbm, ids_hbm, high, low, *refs):
    rest, (own_ref, k_ref, v_ref, q_ref, ids_ref, sem) = refs[: pairs - 1], refs[pairs - 1 :]
    rows = k_ref.shape[0]
    moves = []
    routes = [(k_hbm, k_ref), (v_hbm, v_ref), (q_hbm, q_ref), (ids_hbm, ids_ref)]
    for at, (source, target) in enumerate(routes):
        moves.append(pltpu.make_async_copy(source, target, sem.at[at]))
        moves[-1].start()
    for item in moves:
        item.wait()
    ids = ids_ref[...].astype(jnp.float32)
    own_ref[...] = ids
    wide = jnp.broadcast_to(ids, (TILE, rows))
    odd = is_odd()

    def put(target, pair):
        target[:rows, :] = k_ref[:, cut(pair)].astype(jnp.float32)
        target[rows : 2 * rows, :] = v_ref[:, cut(pair)].astype(jnp.float32)

    def fill(up, down):
        size = up.shape[0] - TILE
        put(up, 0)
        for pair in range(pairs):
            down[pair * rows : (pair + 1) * rows, :] = q_ref[:, cut(pair)].astype(jnp.float32)
        for target, done in ((up, 2 * rows), (down, pairs * rows)):
            if done < size:
                target[done:size, :] = jnp.zeros((size - done, LANES), jnp.float32)
            target[size:, :] = wide

    @pl.when(odd)
    def _():
        fill(high, low)

    @pl.when(jnp.logical_not(odd))
    def _():
        fill(low, high)

    for pair in range(1, pairs):
        put(rest[pair - 1], pair)


def local_body(pairs, q_ref, *refs):
    (high, low, side), (y_ref,) = groups_of(refs, 3, pairs)
    rows = q_ref.shape[0]
    odd = is_odd()
    ids = pick_ids(odd, high[0], low[0])
    row_pos = lax.broadcasted_iota(jnp.int32, (rows, rows), 0)
    col_pos = lax.broadcasted_iota(jnp.int32, (rows, rows), 1)
    tall = jnp.sum(jnp.where(row_pos == col_pos, ids, 0.0), axis=1, keepdims=True)
    allowed = (row_pos >= col_pos) & (tall == ids)
    seen = rows_of_first(ids)
    before = jnp.where(odd, pick_ids(odd, side[0], side[0]), -1.0) == ids[:, 0:1]
    for pair in range(pairs):
        q_two = q_ref[:, cut(pair)]
        near = attend(q_two, *pick_pair(odd, high, low, pair, rows), allowed)
        earlier = attend(q_two, *pick_pair(odd, side, side, pair, rows), before)
        y_ref[pair * rows : (pair + 1) * rows, :] = near + jnp.where(seen, earlier, 0.0)


def finish(y, o_ref, pair):
    low = lower_half(y.shape)
    square = y * y
    sum_low = jnp.sum(jnp.where(low, square, 0.0), axis=1, keepdims=True)
    sum_high = jnp.sum(jnp.where(low, 0.0, square), axis=1, keepdims=True)
    mean = jnp.where(low, sum_low, sum_high) * (1.0 / HW)
    o_ref[:, cut(pair)] = (y * lax.rsqrt(mean + EPS)).astype(o_ref.dtype)


def deliver(o_ref, o_hbm, sem):
    copy = pltpu.make_async_copy(o_ref, o_hbm, sem)
    copy.start()
    copy.wait()


def has_far():
    return lax.axis_index("ctx") >= 4


def near_body(pairs, q_ref, own_ref, y_ref, *refs):
    (high, low, high_side, low_side), (t_ref, o_hbm, o_ref, sem) = groups_of(refs, 4, pairs)
    rows = q_ref.shape[0]
    odd = is_odd()
    usable = lax.axis_index("ctx") >= 2
    ids = own_ref[...]
    seen = rows_of_first(ids)
    sources = ((high, low), (low_side, high_side))
    masks = [
        jnp.where(usable, pick_ids(odd, this[0], other[0]), -1.0) == ids[:, 0:1]
        for this, other in sources
    ]
    for pair in range(pairs):
        q_two = q_ref[:, cut(pair)]
        total = jnp.zeros((rows, LANES), jnp.float32)
        for (this, other), mask in zip(sources, masks, strict=True):
            total = total + attend(q_two, *pick_pair(odd, this, other, pair, rows), mask)
        span = slice(pair * rows, (pair + 1) * rows)
        t_ref[span, :] = y_ref[span, :] + jnp.where(seen, total, 0.0)

    @pl.when(jnp.logical_not(has_far()))
    def _():
        for pair in range(pairs):
            finish(t_ref[pair * rows : (pair + 1) * rows, :], o_ref, pair)
        deliver(o_ref, o_hbm, sem)


def far_body(pair, high0, low0, side0, high, low, side, o_ref):
    rows = o_ref.shape[0]
    odd = is_odd()
    first = pick_ids(odd, low0, high0)[:, 0:1]
    near_mask = pick_ids(odd, high0, low0) == first
    side_mask = jnp.where(odd, -1.0, pick_ids(odd, side0, side0)) == first
    q_two = pick(odd, low0, high0, pair * rows, rows).astype(jnp.bfloat16)
    total = attend(q_two, *pick_pair(odd, [high], [low], 0, rows), near_mask)
    o_ref[...] = total + attend(q_two, *pick_pair(odd, [side], [side], 0, rows), side_mask)


def far_all(pairs, *refs):
    (high, low, side), (o_ref,) = groups_of(refs, 3, pairs)
    rows = o_ref.shape[0] // pairs
    for pair in range(pairs):
        far_body(
            pair, high[0], low[0], side[0], high[pair], low[pair], side[pair],
            o_ref.at[pair * rows : (pair + 1) * rows, :],
        )


def last_body(pairs, own_ref, y_ref, _, *refs):
    far, (o_hbm, o_ref, sem) = refs[: 2 * pairs], refs[2 * pairs :]
    rows = o_ref.shape[0]

    @pl.when(has_far())
    def _():
        odd = is_odd()
        seen = rows_of_first(own_ref[...])
        for pair in range(pairs):
            start = pair * rows if far[0].shape[0] > rows else 0
            came = pick(odd, far[2 * pair], far[2 * pair + 1], start, rows)
            y = y_ref[pair * rows : (pair + 1) * rows, :] + jnp.where(seen, came, 0.0)
            finish(y, o_ref, pair)
        deliver(o_ref, o_hbm, sem)


def call(body, out, flops, *args, **extra):
    moved = sum(a.size * a.dtype.itemsize for a in args)
    return pl.pallas_call(
        body,
        out_shape=out,
        cost_estimate=pl.CostEstimate(flops=flops, bytes_accessed=moved, transcendentals=0),
        compiler_params=pltpu.CompilerParams(vmem_limit_bytes=GRANT),
        **extra,
    )(*args)


def f32(*shape):
    return jax.ShapeDtypeStruct(shape, jnp.float32)


def per_device(queries, keys, values, doc_ids):
    rows, columns = queries.shape
    assert columns % LANES == 0 and rows == LANES and lax.axis_size("ctx") % 2 == 0
    assert MOST <= 4 * rows
    pairs = columns // LANES
    one = 4 * rows * rows * LANES
    ids = doc_ids.reshape(1, rows)
    held = [pltpu.with_memory_space_constraint(x, pltpu.HBM) for x in (keys, values, queries, ids)]
    load = f32(max(2, pairs) * rows + TILE, LANES)
    y_shape = f32(pairs * rows, LANES)
    every = range(pairs)

    def work(body, out, flops, *args):
        return call(functools.partial(body, pairs), out, flops, *args)

    def each(moved, arrays):
        out = []
        for pair in every:
            out.append(None if arrays[pair] is None else moved(arrays[pair]))
        return out

    high, low, *rest, own = call(
        functools.partial(pack_body, pairs),
        (load, load, *[f32(2 * rows, LANES)] * (pairs - 1), f32(1, rows)),
        0,
        *held,
        in_specs=[pl.BlockSpec(memory_space=pltpu.HBM)] * 4,
        scratch_shapes=[pltpu.VMEM((rows, columns), x.dtype) for x in (keys, values, queries)]
        + [pltpu.VMEM((1, rows), ids.dtype), pltpu.SemaphoreType.DMA((4,))],
    )
    highs, lows = [high, *rest], [low, *rest]
    got_high = [snake(high, 1, 0)]
    got_low = [snake(low, 0, 0)]
    for pair in range(1, pairs):
        if UP == "S":
            got_high.append(snake(rest[pair - 1], 1, 0))
            got_low.append(snake(rest[pair - 1], 0, 0))
        else:
            got_high.append((climb if UP == "C" else rise)(rest[pair - 1], 0))
            got_low.append(got_high[-1])
    side = each(trade, lows)
    high_side = each(trade, got_high)
    low_side = []
    for pair in every:
        if pair and UP != "S":
            low_side.append(high_side[pair])
        else:
            low_side.append(trade(got_low[pair]))
    lead = (got_high[0], got_low[0], high_side[0])

    def backs(value, kind):
        if kind == "T":
            one_way = snake(value, 1, 1)
            return [one_way, snake(value, 0, 1)]
        return [(climb if kind == "C" else rise)(value, 1)] * 2

    back = []
    if len(BACK) == 1:
        far = call(
            functools.partial(far_all, pairs), y_shape, 4 * pairs * one,
            *got_high, *got_low, *high_side,
        )
        back = backs(far, BACK) * pairs
    else:
        for pair in every:
            args = (*lead, got_high[pair], got_low[pair], high_side[pair])
            body = functools.partial(far_body, pair)
            far = call(body, f32(rows, LANES), 4 * one, *args)
            back += backs(far, BACK[pair])
    y = work(local_body, y_shape, 4 * pairs * one, queries, *highs, *lows, *side)
    out = jax.ShapeDtypeStruct((rows, columns), queries.dtype)
    staged = [pltpu.VMEM(out.shape, out.dtype), pltpu.SemaphoreType.DMA(())]
    here, there = pl.BlockSpec(memory_space=pltpu.VMEM), pl.BlockSpec(memory_space=pltpu.HBM)
    y, out_so_far = call(
        functools.partial(near_body, pairs),
        (y_shape, out),
        4 * pairs * one,
        queries,
        own,
        y,
        *got_high,
        *got_low,
        *high_side,
        *low_side,
        out_specs=(here, there),
        scratch_shapes=staged,
    )
    return call(
        functools.partial(last_body, pairs),
        out,
        0,
        own,
        y,
        out_so_far,
        *back,
        in_specs=[here, here, there] + [here] * len(back),
        out_specs=there,
        scratch_shapes=staged,
        input_output_aliases={2: 0},
    )


UP = "C"
BACK = 'CC'


def solution(mesh):
    placed = P(("groups", "ctx"), ("heads", "rep"))
    return jax.shard_map(
        per_device,
        mesh=mesh,
        in_specs=(placed, placed, placed, P(("groups", "ctx"))),
        out_specs=placed,
        check_vma=False,
    )
```

time: 20.8 us -> 18.1 us (0.87)
  the two profiles are of different devices: /device:TPU:13 before, /device:TPU:0 now
where the time goes in v2:
time: 18.1 us; the launch traced here: 17.9 us
  waiting for transfers between devices  7.64 us (42%)
  starting transfers between devices  6.71 us (37%)
  Pallas kernels  3.46 us (19%)
    ppermute x3, waiting for transfers between devices, climb(): return lax.ppermute(x, 'ctx', pairs)  6.66 us
    pallas_call x6, Pallas kernels, call(): pl.pallas_call(body, out_shape=out, cost_estimate=pl.CostEstimate(flops=f...  3.46 us
    ppermute x3, starting transfers between devices, climb(): return lax.ppermute(x, 'ctx', pairs)  3.21 us
    ppermute x2, starting transfers between devices, snake(): return lax.ppermute(x, 'ctx', pairs)  2.47 us
    ppermute x5, starting transfers between devices, trade(): lax.ppermute(x, 'ctx', [(i, i ^ 1) for i in range(lax.axis_size('ctx'))])  1.02 us
    ppermute x2, waiting for transfers between devices, snake(): return lax.ppermute(x, 'ctx', pairs)  0.97 us
  transfers between devices with their start and end apart: 10, of which 2 were waited for; matrix products, arithmetic and copies ran while one was open for 0% of the time, Pallas kernels for 14%

profile of v2, /device:TPU:0, one launch (start us, length us, event | category | flops | bytes accessed | tf_op | source)
XLA Modules:
  0.0 17.9 jit_solution(5090489321029129950)
XLA Ops:
  0.0 1.0 %shard_map.46 = (f32[264,128]{1,0:T(8,128)S(1)}, f32[264,128]{1,0:T(8,128)S(1)}, f32[256,128]{1,0:T(8,128)S(1)}, f32[1,128]{1,0:T(1,128)S(1)}) custom-call(bf16[128,256]{1,0:T(8,128)(2,1)} %k_hbm.1, bf16[128,256]{1,0:T(8,128)(2,1)} %v_hbm.1, bf16[128,256]{1,0:T(8,128)(2,1)} %q_ref.3, s32[1,128]{1,0:T(1,128)} %bitcast.1), custom_call_target="tpu_custom_call" | custom-call | bytes 197120 | tf_op jit(solution)/shard_map/pallas_call | solution.py:244
  1.0 0.5 %collective-permute-start.2 = (f32[264,128]{1,0:T(8,128)S(1)}, f32[264,128]{1,0:T(8,128)S(1)}, u32[]{:S(2)}, u32[]{:S(2)}) collective-permute-start(f32[264,128]{1,0:T(8,128)S(1)} %get-tuple-element.12.refs_0_), channel_id=1, source_target_pairs={{2,6},{0,2},{6,10},{4,0},{10,14},{8,4},{14,12},{12,8},{3,7},{1,3},... | collective-permute-start | bytes 405512 | tf_op jit(solution)/shard_map/ppermute | solution.py:26
  1.5 2.6 %collective-permute-start.3 = (f32[256,128]{1,0:T(8,128)S(1)}, f32[256,128]{1,0:T(8,128)S(1)}, u32[]{:S(2)}, u32[]{:S(2)}) collective-permute-start(f32[256,128]{1,0:T(8,128)S(1)} %get-tuple-element.13.refs_1_.refs_3_), channel_id=1, source_target_pairs={{0,4},{2,6},{4,8},{6,10},{8,12},{10,14},{12,0},{14,2},{1,5},{3,7},... | collective-permute-start | bytes 393224 | tf_op jit(solution)/shard_map/ppermute | solution.py:37
  4.1 2.0 %collective-permute-start.4 = (f32[264,128]{1,0:T(8,128)S(1)}, f32[264,128]{1,0:T(8,128)S(1)}, u32[]{:S(2)}, u32[]{:S(2)}) collective-permute-start(f32[264,128]{1,0:T(8,128)S(1)} %get-tuple-element.14.refs_2_), channel_id=1, source_target_pairs={{0,4},{2,0},{4,8},{6,2},{8,12},{10,6},{12,14},{14,10},{1,5},{3,1},... | collective-permute-start | bytes 405512 | tf_op jit(solution)/shard_map/ppermute | solution.py:26
  6.1 1.0 %collective-permute-done.2.refs_0_.high0.high = f32[264,128]{1,0:T(8,128)S(1)} collective-permute-done((f32[264,128]{1,0:T(8,128)S(1)}, f32[264,128]{1,0:T(8,128)S(1)}, u32[]{:S(2)}, u32[]{:S(2)}) %collective-permute-start.2) | collective-permute-done | bytes 135200 | tf_op jit(solution)/shard_map/ppermute | solution.py:26
  7.0 0.0 collective-permute-start.5
  7.0 6.7 %collective-permute-done.3.refs_1_.refs_3_.high.low = f32[256,128]{1,0:T(8,128)S(1)} collective-permute-done((f32[256,128]{1,0:T(8,128)S(1)}, f32[256,128]{1,0:T(8,128)S(1)}, u32[]{:S(2)}, u32[]{:S(2)}) %collective-permute-start.3) | collective-permute-done | bytes 131104 | tf_op jit(solution)/shard_map/ppermute | solution.py:37
  13.7 0.0 collective-permute-start.6
  13.7 0.5 %collective-permute-start = (f32[264,128]{1,0:T(8,128)S(1)}, f32[264,128]{1,0:T(8,128)S(1)}, u32[]{:S(2)}, u32[]{:S(2)}) collective-permute-start(f32[264,128]{1,0:T(8,128)S(1)} %get-tuple-element.14.refs_2_), channel_id=1, source_target_pairs={{0,2},{2,0},{4,6},{6,4},{8,10},{10,8},{12,14},{14,12},{1,3},{3,1},... | collective-permute-start | bytes 405512 | tf_op jit(solution)/shard_map/ppermute | solution.py:46
  14.2 0.0 collective-permute-start.1
  14.2 0.0 collective-permute-done.4.refs_2_.low0.low
  14.2 0.5 %collective-permute-start.7 = (f32[264,128]{1,0:T(8,128)S(1)}, f32[264,128]{1,0:T(8,128)S(1)}, u32[]{:S(2)}, u32[]{:S(2)}) collective-permute-start(f32[264,128]{1,0:T(8,128)S(1)} %collective-permute-done.4.refs_2_.low0.low), channel_id=1, source_target_pairs={{0,2},{2,0},{4,6},{6,4},{8,10},{10,8},{12,14},{14,12},{1,3},{3,1},... | collective-permute-start | bytes 405512 | tf_op jit(solution)/shard_map/ppermute | solution.py:46
  14.7 0.0 collective-permute-done.5.refs_4_.side0.side
  14.7 0.3 %shard_map.49 = f32[128,128]{1,0:T(8,128)S(1)} custom-call(f32[264,128]{1,0:T(8,128)S(1)} %collective-permute-done.2.refs_0_.high0.high, f32[264,128]{1,0:T(8,128)S(1)} %collective-permute-done.4.refs_2_.low0.low, f32[264,128]{1,0:T(8,128)S(1)} %collective-permute-done.5.refs_4_.side0.side, f32[264,128]{1,0:T(8,128)S(1)} %collective-permute-done.2.refs_0_.high0.high, ...), custom_call_target="tpu_custom_call" | custom-call | flops 33554432 | bytes 811008 | tf_op jit(solution)/shard_map/pallas_call | solution.py:244
  15.1 0.0 copy-start
  15.1 0.1 collective-permute-start.8
  15.1 0.0 collective-permute-done.6.refs_5_.refs_7_.side
  15.1 0.3 %shard_map.50 = f32[128,128]{1,0:T(8,128)S(1)} custom-call(f32[264,128]{1,0:T(8,128)S(1)} %collective-permute-done.2.refs_0_.high0.high, f32[264,128]{1,0:T(8,128)S(1)} %collective-permute-done.4.refs_2_.low0.low, f32[264,128]{1,0:T(8,128)S(1)} %collective-permute-done.5.refs_4_.side0.side, f32[256,128]{1,0:T(8,128)S(1)} %collective-permute-done.3.refs_1_.refs_3_.high.low, ...), custom_call_target="tpu_custom_call" | custom-call | flops 33554432 | bytes 798720 | tf_op jit(solution)/shard_map/pallas_call | solution.py:244
  15.5 0.5 %collective-permute-start.9 = (f32[128,128]{1,0:T(8,128)S(1)}, f32[128,128]{1,0:T(8,128)S(1)}, u32[]{:S(2)}, u32[]{:S(2)}) collective-permute-start(f32[128,128]{1,0:T(8,128)S(1)} %shard_map.50), channel_id=1, source_target_pairs={{0,2},{2,0},{4,8},{6,10},{8,12},{10,14},{12,4},{14,6},{1,3},{3,1},... | collective-permute-start | bytes 196616 | tf_op jit(solution)/shard_map/ppermute | solution.py:37
  16.0 0.0 collective-permute-done.1.refs_5_
  16.0 0.0 collective-permute-done.refs_4_
  16.0 0.0 copy-done
  16.0 0.5 %shard_map.47.y_ref = f32[256,128]{1,0:T(8,128)S(1)} custom-call(bf16[128,256]{1,0:T(8,128)(2,1)S(1)} %copy-done, f32[264,128]{1,0:T(8,128)S(1)} %get-tuple-element.12.refs_0_, f32[256,128]{1,0:T(8,128)S(1)} %get-tuple-element.13.refs_1_.refs_3_, f32[264,128]{1,0:T(8,128)S(1)} %get-tuple-element.14.refs_2_, ...), custom_call_target="tpu_custom_call" | custom-call | flops 67108864 | bytes 864256 | tf_op jit(solution)/shard_map/pallas_call | solution.py:244
  16.5 0.0 collective-permute-done.7.refs_6_
  16.5 1.3 %shard_map.48 = (f32[256,128]{1,0:T(8,128)S(1)}, bf16[128,256]{1,0:T(8,128)(2,1)}) custom-call(bf16[128,256]{1,0:T(8,128)(2,1)S(1)} %copy-done, f32[1,128]{1,0:T(1,128)S(1)} %get-tuple-element.11.own_ref, f32[256,128]{1,0:T(8,128)S(1)} %shard_map.47.y_ref, f32[264,128]{1,0:T(8,128)S(1)} %collective-permute-done.2.refs_0_.high0.high, ...), custom_call_target="tpu_custom_call" | custom-call | flops 67108864 | bytes 1262080 | tf_op jit(solution)/shard_map/pallas_call | solution.py:244
  17.9 0.0 collective-permute-done.8.refs_0_.refs_1_
  17.9 0.0 collective-permute-done.9.refs_2_.refs_3_
  (1 shorter events, 0.0 us)
Async XLA Ops:
  1.0 6.1 %collective-permute-start.2 = (f32[264,128]{1,0:T(8,128)S(1)}, f32[264,128]{1,0:T(8,128)S(1)}, u32[]{:S(2)}, u32[]{:S(2)}) collective-permute-start(f32[264,128]{1,0:T(8,128)S(1)} %get-tuple-element.12.refs_0_), channel_id=1, source_target_pairs={{2,6},{0,2},{6,10},{4,0},{10,14},{8,4},{14,12},{12,8},{3,7},{1,3},... | collective-permute-start | bytes 405512 | tf_op jit(solution)/shard_map/ppermute | solution.py:26
  1.5 12.2 %collective-permute-start.3 = (f32[256,128]{1,0:T(8,128)S(1)}, f32[256,128]{1,0:T(8,128)S(1)}, u32[]{:S(2)}, u32[]{:S(2)}) collective-permute-start(f32[256,128]{1,0:T(8,128)S(1)} %get-tuple-element.13.refs_1_.refs_3_), channel_id=1, source_target_pairs={{0,4},{2,6},{4,8},{6,10},{8,12},{10,14},{12,0},{14,2},{1,5},{3,7},... | collective-permute-start | bytes 393224 | tf_op jit(solution)/shard_map/ppermute | solution.py:37
  4.1 10.1 %collective-permute-start.4 = (f32[264,128]{1,0:T(8,128)S(1)}, f32[264,128]{1,0:T(8,128)S(1)}, u32[]{:S(2)}, u32[]{:S(2)}) collective-permute-start(f32[264,128]{1,0:T(8,128)S(1)} %get-tuple-element.14.refs_2_), channel_id=1, source_target_pairs={{0,4},{2,0},{4,8},{6,2},{8,12},{10,6},{12,14},{14,10},{1,5},{3,1},... | collective-permute-start | bytes 405512 | tf_op jit(solution)/shard_map/ppermute | solution.py:26
  7.0 7.7 %collective-permute-start.5 = (f32[264,128]{1,0:T(8,128)S(1)}, f32[264,128]{1,0:T(8,128)S(1)}, u32[]{:S(2)}, u32[]{:S(2)}) collective-permute-start(f32[264,128]{1,0:T(8,128)S(1)} %collective-permute-done.2.refs_0_.high0.high), channel_id=1, source_target_pairs={{0,2},{2,0},{4,6},{6,4},{8,10},{10,8},{12,14},{14,12},{1,3},{3,1},... | collective-permute-start | bytes 405512 | tf_op jit(solution)/shard_map/ppermute | solution.py:46
  13.7 1.4 %collective-permute-start.6 = (f32[256,128]{1,0:T(8,128)S(1)}, f32[256,128]{1,0:T(8,128)S(1)}, u32[]{:S(2)}, u32[]{:S(2)}) collective-permute-start(f32[256,128]{1,0:T(8,128)S(1)} %collective-permute-done.3.refs_1_.refs_3_.high.low), channel_id=1, source_target_pairs={{0,2},{2,0},{4,6},{6,4},{8,10},{10,8},{12,14},{14,12},{1,3},{3,1},... | collective-permute-start | bytes 393224 | tf_op jit(solution)/shard_map/ppermute | solution.py:46
  13.7 2.3 %collective-permute-start = (f32[264,128]{1,0:T(8,128)S(1)}, f32[264,128]{1,0:T(8,128)S(1)}, u32[]{:S(2)}, u32[]{:S(2)}) collective-permute-start(f32[264,128]{1,0:T(8,128)S(1)} %get-tuple-element.14.refs_2_), channel_id=1, source_target_pairs={{0,2},{2,0},{4,6},{6,4},{8,10},{10,8},{12,14},{14,12},{1,3},{3,1},... | collective-permute-start | bytes 405512 | tf_op jit(solution)/shard_map/ppermute | solution.py:46
  14.2 1.8 %collective-permute-start.1 = (f32[256,128]{1,0:T(8,128)S(1)}, f32[256,128]{1,0:T(8,128)S(1)}, u32[]{:S(2)}, u32[]{:S(2)}) collective-permute-start(f32[256,128]{1,0:T(8,128)S(1)} %get-tuple-element.13.refs_1_.refs_3_), channel_id=1, source_target_pairs={{0,2},{2,0},{4,6},{6,4},{8,10},{10,8},{12,14},{14,12},{1,3},{3,1},... | collective-permute-start | bytes 393224 | tf_op jit(solution)/shard_map/ppermute | solution.py:46
  14.2 2.3 %collective-permute-start.7 = (f32[264,128]{1,0:T(8,128)S(1)}, f32[264,128]{1,0:T(8,128)S(1)}, u32[]{:S(2)}, u32[]{:S(2)}) collective-permute-start(f32[264,128]{1,0:T(8,128)S(1)} %collective-permute-done.4.refs_2_.low0.low), channel_id=1, source_target_pairs={{0,2},{2,0},{4,6},{6,4},{8,10},{10,8},{12,14},{14,12},{1,3},{3,1},... | collective-permute-start | bytes 405512 | tf_op jit(solution)/shard_map/ppermute | solution.py:46
  15.1 1.0 %copy-start = (bf16[128,256]{1,0:T(8,128)(2,1)S(1)}, bf16[128,256]{1,0:T(8,128)(2,1)}, u32[]{:S(2)}) copy-start(bf16[128,256]{1,0:T(8,128)(2,1)} %q_ref.3) | copy-start | bytes 196612
  15.1 2.8 %collective-permute-start.8 = (f32[128,128]{1,0:T(8,128)S(1)}, f32[128,128]{1,0:T(8,128)S(1)}, u32[]{:S(2)}, u32[]{:S(2)}) collective-permute-start(f32[128,128]{1,0:T(8,128)S(1)} %shard_map.49), channel_id=1, source_target_pairs={{0,2},{2,0},{4,8},{6,10},{8,12},{10,14},{12,4},{14,6},{1,3},{3,1},... | collective-permute-start | bytes 196616 | tf_op jit(solution)/shard_map/ppermute | solution.py:37
  15.5 2.4 %collective-permute-start.9 = (f32[128,128]{1,0:T(8,128)S(1)}, f32[128,128]{1,0:T(8,128)S(1)}, u32[]{:S(2)}, u32[]{:S(2)}) collective-permute-start(f32[128,128]{1,0:T(8,128)S(1)} %shard_map.50), channel_id=1, source_target_pairs={{0,2},{2,0},{4,8},{6,10},{8,12},{10,14},{12,4},{14,6},{1,3},{3,1},... | collective-permute-start | bytes 196616 | tf_op jit(solution)/shard_map/ppermute | solution.py:37

commit v3 on v2

--- a/solution.py
+++ b/solution.py
@@ -139,7 +139,7 @@
 
 
 def local_body(pairs, q_ref, *refs):
-    (high, low, side), (y_ref,) = groups_of(refs, 3, pairs)
+    (high, low, side), (y_ref, o_hbm, o_ref, sem) = groups_of(refs, 3, pairs)
     rows = q_ref.shape[0]
     odd = is_odd()
     ids = pick_ids(odd, high[0], low[0])
@@ -154,6 +154,7 @@
         near = attend(q_two, *pick_pair(odd, high, low, pair, rows), allowed)
         earlier = attend(q_two, *pick_pair(odd, side, side, pair, rows), before)
         y_ref[pair * rows : (pair + 1) * rows, :] = near + jnp.where(seen, earlier, 0.0)
+    deliver_if(lax.axis_index("ctx") < 2, pairs, y_ref, o_hbm, o_ref, sem)
 
 
 def finish(y, o_ref, pair):
@@ -165,78 +166,73 @@
     o_ref[:, cut(pair)] = (y * lax.rsqrt(mean + EPS)).astype(o_ref.dtype)
 
 
-def deliver(o_ref, o_hbm, sem):
-    copy = pltpu.make_async_copy(o_ref, o_hbm, sem)
-    copy.start()
-    copy.wait()
-
-
-def has_far():
-    return lax.axis_index("ctx") >= 4
-
-
-def near_body(pairs, q_ref, own_ref, y_ref, *refs):
+def deliver_if(wanted, pairs, y_ref, o_hbm, o_ref, sem):
+    rows = o_ref.shape[0]
+
+    @pl.when(wanted)
+    def _():
+        for pair in range(pairs):
+            finish(y_ref[pair * rows : (pair + 1) * rows, :], o_ref, pair)
+        copy = pltpu.make_async_copy(o_ref, o_hbm, sem)
+        copy.start()
+        copy.wait()
+
+
+def near_body(pairs, q_ref, own_ref, y_ref, _, *refs):
     (high, low, high_side, low_side), (t_ref, o_hbm, o_ref, sem) = groups_of(refs, 4, pairs)
     rows = q_ref.shape[0]
     odd = is_odd()
     usable = lax.axis_index("ctx") >= 2
-    ids = own_ref[...]
-    seen = rows_of_first(ids)
-    sources = ((high, low), (low_side, high_side))
-    masks = [
-        jnp.where(usable, pick_ids(odd, this[0], other[0]), -1.0) == ids[:, 0:1]
-        for this, other in sources
-    ]
-    for pair in range(pairs):
-        q_two = q_ref[:, cut(pair)]
-        total = jnp.zeros((rows, LANES), jnp.float32)
-        for (this, other), mask in zip(sources, masks, strict=True):
-            total = total + attend(q_two, *pick_pair(odd, this, other, pair, rows), mask)
-        span = slice(pair * rows, (pair + 1) * rows)
-        t_ref[span, :] = y_ref[span, :] + jnp.where(seen, total, 0.0)
-
-    @pl.when(jnp.logical_not(has_far()))
-    def _():
+
+    @pl.when(usable)
+    def _():
+        ids = own_ref[...]
+        seen = rows_of_first(ids)
+        sources = ((high, low), (low_side, high_side))
+        masks = [
+            jnp.where(usable, pick_ids(odd, this[0], other[0]), -1.0) == ids[:, 0:1]
+            for this, other in sources
+        ]
         for pair in range(pairs):
-            finish(t_ref[pair * rows : (pair + 1) * rows, :], o_ref, pair)
-        deliver(o_ref, o_hbm, sem)
+            q_two = q_ref[:, cut(pair)]
+            total = jnp.zeros((rows, LANES), jnp.float32)
+            for (this, other), mask in zip(sources, masks, strict=True):
+                total = total + attend(q_two, *pick_pair(odd, this, other, pair, rows), mask)
+            span = slice(pair * rows, (pair + 1) * rows)
+            t_ref[span, :] = y_ref[span, :] + jnp.where(seen, total, 0.0)
+
+    here = lax.axis_index("ctx")
+    deliver_if((here >= 2) & (here < 4), pairs, t_ref, o_hbm, o_ref, sem)
 
 
 def far_body(pair, high0, low0, side0, high, low, side, o_ref):
     rows = o_ref.shape[0]
     odd = is_odd()
-    first = pick_ids(odd, low0, high0)[:, 0:1]
-    near_mask = pick_ids(odd, high0, low0) == first
-    side_mask = jnp.where(odd, -1.0, pick_ids(odd, side0, side0)) == first
-    q_two = pick(odd, low0, high0, pair * rows, rows).astype(jnp.bfloat16)
-    total = attend(q_two, *pick_pair(odd, [high], [low], 0, rows), near_mask)
-    o_ref[...] = total + attend(q_two, *pick_pair(odd, [side], [side], 0, rows), side_mask)
-
-
-def far_all(pairs, *refs):
-    (high, low, side), (o_ref,) = groups_of(refs, 3, pairs)
-    rows = o_ref.shape[0] // pairs
-    for pair in range(pairs):
-        far_body(
-            pair, high[0], low[0], side[0], high[pair], low[pair], side[pair],
-            o_ref.at[pair * rows : (pair + 1) * rows, :],
-        )
-
-
-def last_body(pairs, own_ref, y_ref, _, *refs):
-    far, (o_hbm, o_ref, sem) = refs[: 2 * pairs], refs[2 * pairs :]
+    here = lax.axis_index("ctx")
+
+    @pl.when((here >= 2) & (here < lax.axis_size("ctx") - 2))
+    def _():
+        first = pick_ids(odd, low0, high0)[:, 0:1]
+        near_mask = pick_ids(odd, high0, low0) == first
+        side_mask = jnp.where(odd, -1.0, pick_ids(odd, side0, side0)) == first
+        q_two = pick(odd, low0, high0, pair * rows, rows).astype(jnp.bfloat16)
+        total = attend(q_two, *pick_pair(odd, [high], [low], 0, rows), near_mask)
+        o_ref[...] = total + attend(q_two, *pick_pair(odd, [side], [side], 0, rows), side_mask)
+
+
+def last_body(pair, own_ref, y_ref, _, high, low, o_hbm, o_ref, sem):
     rows = o_ref.shape[0]
-
-    @pl.when(has_far())
-    def _():
-        odd = is_odd()
+    odd = is_odd()
+
+    @pl.when(lax.axis_index("ctx") >= 4)
+    def _():
         seen = rows_of_first(own_ref[...])
-        for pair in range(pairs):
-            start = pair * rows if far[0].shape[0] > rows else 0
-            came = pick(odd, far[2 * pair], far[2 * pair + 1], start, rows)
-            y = y_ref[pair * rows : (pair + 1) * rows, :] + jnp.where(seen, came, 0.0)
-            finish(y, o_ref, pair)
-        deliver(o_ref, o_hbm, sem)
+        came = pick(odd, high, low, 0, rows)
+        y = y_ref[pair * rows : (pair + 1) * rows, :] + jnp.where(seen, came, 0.0)
+        finish(y, o_ref, 0)
+        copy = pltpu.make_async_copy(o_ref, o_hbm.at[:, cut(pair)], sem)
+        copy.start()
+        copy.wait()
 
 
 def call(body, out, flops, *args, **extra):
@@ -265,9 +261,6 @@
     load = f32(max(2, pairs) * rows + TILE, LANES)
     y_shape = f32(pairs * rows, LANES)
     every = range(pairs)
-
-    def work(body, out, flops, *args):
-        return call(functools.partial(body, pairs), out, flops, *args)
 
     def each(moved, arrays):
         out = []
@@ -323,41 +316,56 @@
             body = functools.partial(far_body, pair)
             far = call(body, f32(rows, LANES), 4 * one, *args)
             back += backs(far, BACK[pair])
-    y = work(local_body, y_shape, 4 * pairs * one, queries, *highs, *lows, *side)
     out = jax.ShapeDtypeStruct((rows, columns), queries.dtype)
     staged = [pltpu.VMEM(out.shape, out.dtype), pltpu.SemaphoreType.DMA(())]
     here, there = pl.BlockSpec(memory_space=pltpu.VMEM), pl.BlockSpec(memory_space=pltpu.HBM)
-    y, out_so_far = call(
+    y, partly = call(
+        functools.partial(local_body, pairs),
+        (y_shape, out),
+        4 * pairs * one,
+        queries,
+        *highs,
+        *lows,
+        *side,
+        out_specs=(here, there),
+        scratch_shapes=staged,
+    )
+    y, partly = call(
         functools.partial(near_body, pairs),
         (y_shape, out),
         4 * pairs * one,
         queries,
         own,
         y,
+        partly,
         *got_high,
         *got_low,
         *high_side,
         *low_side,
+        in_specs=[here] * 3 + [there] + [here] * (4 * pairs),
         out_specs=(here, there),
         scratch_shapes=staged,
-    )
-    return call(
-        functools.partial(last_body, pairs),
-        out,
-        0,
-        own,
-        y,
-        out_so_far,
-        *back,
-        in_specs=[here, here, there] + [here] * len(back),
-        out_specs=there,
-        scratch_shapes=staged,
-        input_output_aliases={2: 0},
-    )
+        input_output_aliases={3: 1},
+    )
+    for pair in every:
+        partly = call(
+            functools.partial(last_body, pair),
+            out,
+            0,
+            own,
+            y,
+            partly,
+            *back[2 * pair : 2 * pair + 2],
+            in_specs=[here, here, there, here, here],
+            out_specs=there,
+            scratch_shapes=[pltpu.VMEM((rows, LANES), out.dtype), staged[1]],
+            input_output_aliases={2: 0},
+        )
+    return partly
 
 
 UP = "C"
-BACK = 'CC'
+BACK = "CC"
 
 
 def solution(mesh):

time: 18.1 us -> 17.7 us (0.978)
  the two profiles are of different devices: /device:TPU:0 before, /device:TPU:10 now
where the time goes in v3:
time: 17.7 us; the launch traced here: 17.5 us
  starting transfers between devices  7.07 us (40%)
  waiting for transfers between devices  6.87 us (39%)
  Pallas kernels  3.47 us (20%)
    ppermute x3, starting transfers between devices, climb(): return lax.ppermute(x, 'ctx', pairs)  4.4 us
    pallas_call x7, Pallas kernels, call(): pl.pallas_call(body, out_shape=out, cost_estimate=pl.CostEstimate(flops=f...  3.47 us
    ppermute x2, waiting for transfers between devices, snake(): return lax.ppermute(x, 'ctx', pairs)  3.45 us
    ppermute x3, waiting for transfers between devices, climb(): return lax.ppermute(x, 'ctx', pairs)  3.41 us
    ppermute x2, starting transfers between devices, snake(): return lax.ppermute(x, 'ctx', pairs)  2.04 us
    ppermute x5, starting transfers between devices, trade(): lax.ppermute(x, 'ctx', [(i, i ^ 1) for i in range(lax.axis_size('ctx'))])  0.63 us
  transfers between devices with their start and end apart: 10, of which 5 were waited for; matrix products, arithmetic and copies ran while one was open for 0% of the time, Pallas kernels for 14%

profile of v3, /device:TPU:10, one launch (start us, length us, event | category | flops | bytes accessed | tf_op | source)
XLA Modules:
  0.0 17.5 jit_solution(9037660127721122496)
XLA Ops:
  0.0 1.0 %shard_map.46 = (f32[264,128]{1,0:T(8,128)S(1)}, f32[264,128]{1,0:T(8,128)S(1)}, f32[256,128]{1,0:T(8,128)S(1)}, f32[1,128]{1,0:T(1,128)S(1)}) custom-call(bf16[128,256]{1,0:T(8,128)(2,1)} %k_hbm.1, bf16[128,256]{1,0:T(8,128)(2,1)} %v_hbm.1, bf16[128,256]{1,0:T(8,128)(2,1)} %q_ref.3, s32[1,128]{1,0:T(1,128)} %bitcast.1), custom_call_target="tpu_custom_call" | custom-call | bytes 197120 | tf_op jit(solution)/shard_map/pallas_call | solution.py:240
  1.0 0.5 %collective-permute-start.2 = (f32[264,128]{1,0:T(8,128)S(1)}, f32[264,128]{1,0:T(8,128)S(1)}, u32[]{:S(2)}, u32[]{:S(2)}) collective-permute-start(f32[264,128]{1,0:T(8,128)S(1)} %get-tuple-element.14.refs_0_), channel_id=1, source_target_pairs={{2,6},{0,2},{6,10},{4,0},{10,14},{8,4},{14,12},{12,8},{3,7},{1,3},... | collective-permute-start | bytes 405512 | tf_op jit(solution)/shard_map/ppermute | solution.py:26
  1.4 1.6 %collective-permute-start.3 = (f32[256,128]{1,0:T(8,128)S(1)}, f32[256,128]{1,0:T(8,128)S(1)}, u32[]{:S(2)}, u32[]{:S(2)}) collective-permute-start(f32[256,128]{1,0:T(8,128)S(1)} %get-tuple-element.15.refs_1_.refs_3_), channel_id=1, source_target_pairs={{0,4},{2,6},{4,8},{6,10},{8,12},{10,14},{12,0},{14,2},{1,5},{3,7},... | collective-permute-start | bytes 393224 | tf_op jit(solution)/shard_map/ppermute | solution.py:37
  3.0 1.6 %collective-permute-start.4 = (f32[264,128]{1,0:T(8,128)S(1)}, f32[264,128]{1,0:T(8,128)S(1)}, u32[]{:S(2)}, u32[]{:S(2)}) collective-permute-start(f32[264,128]{1,0:T(8,128)S(1)} %get-tuple-element.16.refs_2_), channel_id=1, source_target_pairs={{0,4},{2,0},{4,8},{6,2},{8,12},{10,6},{12,14},{14,10},{1,5},{3,1},... | collective-permute-start | bytes 405512 | tf_op jit(solution)/shard_map/ppermute | solution.py:26
  4.6 2.5 %collective-permute-done.2.refs_0_.high0.high = f32[264,128]{1,0:T(8,128)S(1)} collective-permute-done((f32[264,128]{1,0:T(8,128)S(1)}, f32[264,128]{1,0:T(8,128)S(1)}, u32[]{:S(2)}, u32[]{:S(2)}) %collective-permute-start.2) | collective-permute-done | bytes 135200 | tf_op jit(solution)/shard_map/ppermute | solution.py:26
  7.1 0.0 collective-permute-start.5
  7.1 0.6 %collective-permute-done.3.refs_1_.refs_3_.high.low = f32[256,128]{1,0:T(8,128)S(1)} collective-permute-done((f32[256,128]{1,0:T(8,128)S(1)}, f32[256,128]{1,0:T(8,128)S(1)}, u32[]{:S(2)}, u32[]{:S(2)}) %collective-permute-start.3) | collective-permute-done | bytes 131104 | tf_op jit(solution)/shard_map/ppermute | solution.py:37
  7.7 0.0 collective-permute-start.6
  7.7 0.5 %collective-permute-start = (f32[264,128]{1,0:T(8,128)S(1)}, f32[264,128]{1,0:T(8,128)S(1)}, u32[]{:S(2)}, u32[]{:S(2)}) collective-permute-start(f32[264,128]{1,0:T(8,128)S(1)} %get-tuple-element.16.refs_2_), channel_id=1, source_target_pairs={{0,2},{2,0},{4,6},{6,4},{8,10},{10,8},{12,14},{14,12},{1,3},{3,1},... | collective-permute-start | bytes 405512 | tf_op jit(solution)/shard_map/ppermute | solution.py:46
  8.2 0.0 collective-permute-start.1
  8.2 0.9 %collective-permute-done.4.refs_2_.low0.low = f32[264,128]{1,0:T(8,128)S(1)} collective-permute-done((f32[264,128]{1,0:T(8,128)S(1)}, f32[264,128]{1,0:T(8,128)S(1)}, u32[]{:S(2)}, u32[]{:S(2)}) %collective-permute-start.4) | collective-permute-done | bytes 135200 | tf_op jit(solution)/shard_map/ppermute | solution.py:26
  9.1 0.1 collective-permute-start.7
  9.2 0.0 collective-permute-done.5.refs_4_.side0.side
  9.2 0.3 %shard_map.49 = f32[128,128]{1,0:T(8,128)S(1)} custom-call(f32[264,128]{1,0:T(8,128)S(1)} %collective-permute-done.2.refs_0_.high0.high, f32[264,128]{1,0:T(8,128)S(1)} %collective-permute-done.4.refs_2_.low0.low, f32[264,128]{1,0:T(8,128)S(1)} %collective-permute-done.5.refs_4_.side0.side, f32[264,128]{1,0:T(8,128)S(1)} %collective-permute-done.2.refs_0_.high0.high, ...), custom_call_target="tpu_custom_call" | custom-call | flops 33554432 | bytes 811008 | tf_op jit(solution)/shard_map/pallas_call | solution.py:240
  9.6 0.0 copy-start
  9.6 2.3 %collective-permute-start.8 = (f32[128,128]{1,0:T(8,128)S(1)}, f32[128,128]{1,0:T(8,128)S(1)}, u32[]{:S(2)}, u32[]{:S(2)}) collective-permute-start(f32[128,128]{1,0:T(8,128)S(1)} %shard_map.49), channel_id=1, source_target_pairs={{0,2},{2,0},{4,8},{6,10},{8,12},{10,14},{12,4},{14,6},{1,3},{3,1},... | collective-permute-start | bytes 196616 | tf_op jit(solution)/shard_map/ppermute | solution.py:37
  11.9 0.0 collective-permute-done.6.refs_5_.refs_7_.side
  11.9 0.3 %shard_map.51 = f32[128,128]{1,0:T(8,128)S(1)} custom-call(f32[264,128]{1,0:T(8,128)S(1)} %collective-permute-done.2.refs_0_.high0.high, f32[264,128]{1,0:T(8,128)S(1)} %collective-permute-done.4.refs_2_.low0.low, f32[264,128]{1,0:T(8,128)S(1)} %collective-permute-done.5.refs_4_.side0.side, f32[256,128]{1,0:T(8,128)S(1)} %collective-permute-done.3.refs_1_.refs_3_.high.low, ...), custom_call_target="tpu_custom_call" | custom-call | flops 33554432 | bytes 798720 | tf_op jit(solution)/shard_map/pallas_call | solution.py:240
  12.3 0.5 %collective-permute-start.9 = (f32[128,128]{1,0:T(8,128)S(1)}, f32[128,128]{1,0:T(8,128)S(1)}, u32[]{:S(2)}, u32[]{:S(2)}) collective-permute-start(f32[128,128]{1,0:T(8,128)S(1)} %shard_map.51), channel_id=1, source_target_pairs={{0,2},{2,0},{4,8},{6,10},{8,12},{10,14},{12,4},{14,6},{1,3},{3,1},... | collective-permute-start | bytes 196616 | tf_op jit(solution)/shard_map/ppermute | solution.py:37
  12.7 0.0 collective-permute-done.1.refs_5_
  12.7 0.0 collective-permute-done.refs_4_
  12.8 0.0 copy-done
  12.8 0.5 %shard_map.47 = (f32[256,128]{1,0:T(8,128)S(1)}, bf16[128,256]{1,0:T(8,128)(2,1)}) custom-call(bf16[128,256]{1,0:T(8,128)(2,1)S(1)} %copy-done, f32[264,128]{1,0:T(8,128)S(1)} %get-tuple-element.14.refs_0_, f32[256,128]{1,0:T(8,128)S(1)} %get-tuple-element.15.refs_1_.refs_3_, f32[264,128]{1,0:T(8,128)S(1)} %get-tuple-element.16.refs_2_, ...), custom_call_target="tpu_custom_call" | custom-call | flops 67108864 | bytes 864256 | tf_op jit(solution)/shard_map/pallas_call | solution.py:240
  13.3 0.0 collective-permute-done.7.refs_6_
  13.3 1.3 %shard_map.48 = (f32[256,128]{1,0:T(8,128)S(1)}, bf16[128,256]{1,0:T(8,128)(2,1)}) custom-call(bf16[128,256]{1,0:T(8,128)(2,1)S(1)} %copy-done, f32[1,128]{1,0:T(1,128)S(1)} %get-tuple-element.13.own_ref, f32[256,128]{1,0:T(8,128)S(1)} %get-tuple-element.17.y_ref, bf16[128,256]{1,0:T(8,128)(2,1)} %get-tuple-element.18._, ...), custom_call_target="tpu_custom_call", output_to_operand_aliasing={{1}: (3, {})} | custom-call | flops 67108864 | bytes 1327616 | tf_op jit(solution)/shard_map/pallas_call | solution.py:240
  14.6 0.3 %collective-permute-done.8.high.low = f32[128,128]{1,0:T(8,128)S(1)} collective-permute-done((f32[128,128]{1,0:T(8,128)S(1)}, f32[128,128]{1,0:T(8,128)S(1)}, u32[]{:S(2)}, u32[]{:S(2)}) %collective-permute-start.8) | collective-permute-done | bytes 65568 | tf_op jit(solution)/shard_map/ppermute | solution.py:37
  14.9 2.5 %collective-permute-done.9.high.low = f32[128,128]{1,0:T(8,128)S(1)} collective-permute-done((f32[128,128]{1,0:T(8,128)S(1)}, f32[128,128]{1,0:T(8,128)S(1)}, u32[]{:S(2)}, u32[]{:S(2)}) %collective-permute-start.9) | collective-permute-done | bytes 65568 | tf_op jit(solution)/shard_map/ppermute | solution.py:37
  (2 shorter events, 0.0 us)
Async XLA Ops:
  1.0 6.1 %collective-permute-start.2 = (f32[264,128]{1,0:T(8,128)S(1)}, f32[264,128]{1,0:T(8,128)S(1)}, u32[]{:S(2)}, u32[]{:S(2)}) collective-permute-start(f32[264,128]{1,0:T(8,128)S(1)} %get-tuple-element.14.refs_0_), channel_id=1, source_target_pairs={{2,6},{0,2},{6,10},{4,0},{10,14},{8,4},{14,12},{12,8},{3,7},{1,3},... | collective-permute-start | bytes 405512 | tf_op jit(solution)/shard_map/ppermute | solution.py:26
  1.4 6.2 %collective-permute-start.3 = (f32[256,128]{1,0:T(8,128)S(1)}, f32[256,128]{1,0:T(8,128)S(1)}, u32[]{:S(2)}, u32[]{:S(2)}) collective-permute-start(f32[256,128]{1,0:T(8,128)S(1)} %get-tuple-element.15.refs_1_.refs_3_), channel_id=1, source_target_pairs={{0,4},{2,6},{4,8},{6,10},{8,12},{10,14},{12,0},{14,2},{1,5},{3,7},... | collective-permute-start | bytes 393224 | tf_op jit(solution)/shard_map/ppermute | solution.py:37
  3.0 6.1 %collective-permute-start.4 = (f32[264,128]{1,0:T(8,128)S(1)}, f32[264,128]{1,0:T(8,128)S(1)}, u32[]{:S(2)}, u32[]{:S(2)}) collective-permute-start(f32[264,128]{1,0:T(8,128)S(1)} %get-tuple-element.16.refs_2_), channel_id=1, source_target_pairs={{0,4},{2,0},{4,8},{6,2},{8,12},{10,6},{12,14},{14,10},{1,5},{3,1},... | collective-permute-start | bytes 405512 | tf_op jit(solution)/shard_map/ppermute | solution.py:26
  7.1 2.1 %collective-permute-start.5 = (f32[264,128]{1,0:T(8,128)S(1)}, f32[264,128]{1,0:T(8,128)S(1)}, u32[]{:S(2)}, u32[]{:S(2)}) collective-permute-start(f32[264,128]{1,0:T(8,128)S(1)} %collective-permute-done.2.refs_0_.high0.high), channel_id=1, source_target_pairs={{0,2},{2,0},{4,6},{6,4},{8,10},{10,8},{12,14},{14,12},{1,3},{3,1},... | collective-permute-start | bytes 405512 | tf_op jit(solution)/shard_map/ppermute | solution.py:46
  7.7 4.3 %collective-permute-start.6 = (f32[256,128]{1,0:T(8,128)S(1)}, f32[256,128]{1,0:T(8,128)S(1)}, u32[]{:S(2)}, u32[]{:S(2)}) collective-permute-start(f32[256,128]{1,0:T(8,128)S(1)} %collective-permute-done.3.refs_1_.refs_3_.high.low), channel_id=1, source_target_pairs={{0,2},{2,0},{4,6},{6,4},{8,10},{10,8},{12,14},{14,12},{1,3},{3,1},... | collective-permute-start | bytes 393224 | tf_op jit(solution)/shard_map/ppermute | solution.py:46
  7.7 5.1 %collective-permute-start = (f32[264,128]{1,0:T(8,128)S(1)}, f32[264,128]{1,0:T(8,128)S(1)}, u32[]{:S(2)}, u32[]{:S(2)}) collective-permute-start(f32[264,128]{1,0:T(8,128)S(1)} %get-tuple-element.16.refs_2_), channel_id=1, source_target_pairs={{0,2},{2,0},{4,6},{6,4},{8,10},{10,8},{12,14},{14,12},{1,3},{3,1},... | collective-permute-start | bytes 405512 | tf_op jit(solution)/shard_map/ppermute | solution.py:46
  8.2 4.6 %collective-permute-start.1 = (f32[256,128]{1,0:T(8,128)S(1)}, f32[256,128]{1,0:T(8,128)S(1)}, u32[]{:S(2)}, u32[]{:S(2)}) collective-permute-start(f32[256,128]{1,0:T(8,128)S(1)} %get-tuple-element.15.refs_1_.refs_3_), channel_id=1, source_target_pairs={{0,2},{2,0},{4,6},{6,4},{8,10},{10,8},{12,14},{14,12},{1,3},{3,1},... | collective-permute-start | bytes 393224 | tf_op jit(solution)/shard_map/ppermute | solution.py:46
  9.1 4.2 %collective-permute-start.7 = (f32[264,128]{1,0:T(8,128)S(1)}, f32[264,128]{1,0:T(8,128)S(1)}, u32[]{:S(2)}, u32[]{:S(2)}) collective-permute-start(f32[264,128]{1,0:T(8,128)S(1)} %collective-permute-done.4.refs_2_.low0.low), channel_id=1, source_target_pairs={{0,2},{2,0},{4,6},{6,4},{8,10},{10,8},{12,14},{14,12},{1,3},{3,1},... | collective-permute-start | bytes 405512 | tf_op jit(solution)/shard_map/ppermute | solution.py:46
  9.6 3.2 %copy-start = (bf16[128,256]{1,0:T(8,128)(2,1)S(1)}, bf16[128,256]{1,0:T(8,128)(2,1)}, u32[]{:S(2)}) copy-start(bf16[128,256]{1,0:T(8,128)(2,1)} %q_ref.3) | copy-start | bytes 196612
  9.6 5.3 %collective-permute-start.8 = (f32[128,128]{1,0:T(8,128)S(1)}, f32[128,128]{1,0:T(8,128)S(1)}, u32[]{:S(2)}, u32[]{:S(2)}) collective-permute-start(f32[128,128]{1,0:T(8,128)S(1)} %shard_map.49), channel_id=1, source_target_pairs={{0,2},{2,0},{4,8},{6,10},{8,12},{10,14},{12,4},{14,6},{1,3},{3,1},... | collective-permute-start | bytes 196616 | tf_op jit(solution)/shard_map/ppermute | solution.py:37
  12.3 5.2 %collective-permute-start.9 = (f32[128,128]{1,0:T(8,128)S(1)}, f32[128,128]{1,0:T(8,128)S(1)}, u32[]{:S(2)}, u32[]{:S(2)}) collective-permute-start(f32[128,128]{1,0:T(8,128)S(1)} %shard_map.51), channel_id=1, source_target_pairs={{0,2},{2,0},{4,8},{6,10},{8,12},{10,14},{12,4},{14,6},{1,3},{3,1},... | collective-permute-start | bytes 196616 | tf_op jit(solution)/shard_map/ppermute | solution.py:37

commit v4 on v3

--- a/solution.py
+++ b/solution.py
@@ -16,30 +16,35 @@
 GRANT = 16 << 20
 
 
-def snake(x, rising, first):
+def snake(x, rising):
     couples = lax.axis_size("ctx") // 2
     pairs = []
     for couple in range(couples):
         up, down = 2 * couple + rising, 2 * couple + 1 - rising
-        pairs.append((up, up + 2 if first <= couple < couples - 1 else down))
-        pairs.append((down, down - 2 if couple > first else up))
+        pairs.append((up, up + 2 if couple < couples - 1 else down))
+        pairs.append((down, down - 2 if couple > 0 else up))
     return lax.ppermute(x, "ctx", pairs)
 
 
-def climb(x, first):
+def climb(x, first, stop):
+    pairs = []
+    for couple in range(lax.axis_size("ctx") // 2):
+        for side in range(2):
+            here, stay = 2 * couple + side, not first <= couple < stop or stop - first < 2
+            target = couple + 1 if couple + 1 < stop else first
+            pairs.append((here, here ^ 1 if stay else 2 * target + side))
+    return lax.ppermute(x, "ctx", pairs)
+
+
+def exchange(x, first):
     couples = lax.axis_size("ctx") // 2
     pairs = []
-    for couple in range(couples):
-        for side in range(2):
-            here, stay = 2 * couple + side, couple < first or couples - first < 2
-            target = couple + 1 if couple + 1 < couples else first
-            pairs.append((here, here ^ 1 if stay else 2 * target + side))
+    for here in range(2 * couples):
+        couple = here // 2
+        other = couple + 1 if (couple - first) % 2 == 0 else couple - 1
+        met = couple >= first and first <= other < couples
+        pairs.append((here, 2 * other + here % 2 if met else here ^ 1))
     return lax.ppermute(x, "ctx", pairs)
-
-
-def rise(x, first):
-    length = lax.axis_size("ctx")
-    return lax.ppermute(x, "ctx", [(i, i + 2) for i in range(2 * first, length - 2)])
 
 
 def trade(x):
@@ -178,7 +183,7 @@
         copy.wait()
 
 
-def near_body(pairs, q_ref, own_ref, y_ref, _, *refs):
+def near_body(stop, pairs, q_ref, own_ref, y_ref, _, *refs):
     (high, low, high_side, low_side), (t_ref, o_hbm, o_ref, sem) = groups_of(refs, 4, pairs)
     rows = q_ref.shape[0]
     odd = is_odd()
@@ -193,10 +198,12 @@
             jnp.where(usable, pick_ids(odd, this[0], other[0]), -1.0) == ids[:, 0:1]
             for this, other in sources
         ]
+        below = lax.axis_index("ctx") < 2 * stop
         for pair in range(pairs):
             q_two = q_ref[:, cut(pair)]
             total = jnp.zeros((rows, LANES), jnp.float32)
             for (this, other), mask in zip(sources, masks, strict=True):
+                mask = mask if pair == 0 else mask & below
                 total = total + attend(q_two, *pick_pair(odd, this, other, pair, rows), mask)
             span = slice(pair * rows, (pair + 1) * rows)
             t_ref[span, :] = y_ref[span, :] + jnp.where(seen, total, 0.0)
@@ -205,7 +212,21 @@
     deliver_if((here >= 2) & (here < 4), pairs, t_ref, o_hbm, o_ref, sem)
 
 
-def far_body(pair, high0, low0, side0, high, low, side, o_ref):
+def top_body(stop, pair, high0, low0, own_ref, side0, mine, side, o_ref):
+    rows = o_ref.shape[0]
+    odd = is_odd()
+
+    @pl.when(lax.axis_index("ctx") // 2 == stop - 1)
+    def _():
+        first = pick_ids(odd, low0, high0)[:, 0:1]
+        q_two = pick(odd, low0, high0, pair * rows, rows).astype(jnp.bfloat16)
+        total = attend(q_two, mine[:rows, :], mine[rows : 2 * rows, :], own_ref[...] == first)
+        mask = pick_ids(odd, side0, side0) == first
+        o_ref[...] = total + attend(q_two, side[:rows, :], side[rows : 2 * rows, :], mask)
+
+
+def far_body(stop, pair, high0, low0, side0, high, low, side, *refs):
+    o_ref = refs[-1]
     rows = o_ref.shape[0]
     odd = is_odd()
     here = lax.axis_index("ctx")
@@ -217,18 +238,23 @@
         side_mask = jnp.where(odd, -1.0, pick_ids(odd, side0, side0)) == first
         q_two = pick(odd, low0, high0, pair * rows, rows).astype(jnp.bfloat16)
         total = attend(q_two, *pick_pair(odd, [high], [low], 0, rows), near_mask)
-        o_ref[...] = total + attend(q_two, *pick_pair(odd, [side], [side], 0, rows), side_mask)
-
-
-def last_body(pair, own_ref, y_ref, _, high, low, o_hbm, o_ref, sem):
+        total = total + attend(q_two, *pick_pair(odd, [side], [side], 0, rows), side_mask)
+        if len(refs) > 1:
+            total = total + jnp.where(here // 2 == stop - 1, refs[0][...], 0.0)
+        o_ref[...] = total
+
+
+def last_body(pair, parity, own_ref, y_ref, _, came, o_hbm, o_ref, sem):
     rows = o_ref.shape[0]
-    odd = is_odd()
-
-    @pl.when(lax.axis_index("ctx") >= 4)
+    couple = lax.axis_index("ctx") // 2
+    wanted = couple >= 2
+    if parity is not None:
+        wanted = wanted & (couple % 2 == parity)
+
+    @pl.when(wanted)
     def _():
         seen = rows_of_first(own_ref[...])
-        came = pick(odd, high, low, 0, rows)
-        y = y_ref[pair * rows : (pair + 1) * rows, :] + jnp.where(seen, came, 0.0)
+        y = y_ref[pair * rows : (pair + 1) * rows, :] + jnp.where(seen, came[...], 0.0)
         finish(y, o_ref, 0)
         copy = pltpu.make_async_copy(o_ref, o_hbm.at[:, cut(pair)], sem)
         copy.start()
@@ -261,6 +287,8 @@
     load = f32(max(2, pairs) * rows + TILE, LANES)
     y_shape = f32(pairs * rows, LANES)
     every = range(pairs)
+    couples = lax.axis_size("ctx") // 2
+    stop = couples - 1 if couples > 2 else couples
 
     def each(moved, arrays):
         out = []
@@ -278,44 +306,29 @@
         + [pltpu.VMEM((1, rows), ids.dtype), pltpu.SemaphoreType.DMA((4,))],
     )
     highs, lows = [high, *rest], [low, *rest]
-    got_high = [snake(high, 1, 0)]
-    got_low = [snake(low, 0, 0)]
-    for pair in range(1, pairs):
-        if UP == "S":
-            got_high.append(snake(rest[pair - 1], 1, 0))
-            got_low.append(snake(rest[pair - 1], 0, 0))
-        else:
-            got_high.append((climb if UP == "C" else rise)(rest[pair - 1], 0))
-            got_low.append(got_high[-1])
+    got_high = [snake(high, 1)]
+    got_low = [snake(low, 0)]
+    got = each(lambda x: climb(x, 0, stop), [None, *rest])[1:]
+    got_high, got_low = got_high + got, got_low + got
     side = each(trade, lows)
     high_side = each(trade, got_high)
-    low_side = []
+    low_side = [trade(got_low[0]), *high_side[1:]]
+    lead = (got_high[0], got_low[0])
+    back = []
     for pair in every:
-        if pair and UP != "S":
-            low_side.append(high_side[pair])
+        extra = []
+        if pair and stop < couples:
+            args = (*lead, own, side[0], rest[pair - 1], side[pair])
+            body = functools.partial(top_body, stop, pair)
+            extra = [call(body, f32(rows, LANES), 4 * one, *args)]
+        args = (*lead, high_side[0], got_high[pair], got_low[pair], high_side[pair], *extra)
+        body = functools.partial(far_body, stop, pair)
+        far = call(body, f32(rows, LANES), 4 * one, *args)
+        if pair < pairs - 1:
+            back.append([(None, climb(far, 1, couples))])
         else:
-            low_side.append(trade(got_low[pair]))
-    lead = (got_high[0], got_low[0], high_side[0])
-
-    def backs(value, kind):
-        if kind == "T":
-            one_way = snake(value, 1, 1)
-            return [one_way, snake(value, 0, 1)]
-        return [(climb if kind == "C" else rise)(value, 1)] * 2
-
-    back = []
-    if len(BACK) == 1:
-        far = call(
-            functools.partial(far_all, pairs), y_shape, 4 * pairs * one,
-            *got_high, *got_low, *high_side,
-        )
-        back = backs(far, BACK) * pairs
-    else:
-        for pair in every:
-            args = (*lead, got_high[pair], got_low[pair], high_side[pair])
-            body = functools.partial(far_body, pair)
-            far = call(body, f32(rows, LANES), 4 * one, *args)
-            back += backs(far, BACK[pair])
+            evens = exchange(far, 1)
+            back.append([(0, evens), (1, exchange(far, 2))])
     out = jax.ShapeDtypeStruct((rows, columns), queries.dtype)
     staged = [pltpu.VMEM(out.shape, out.dtype), pltpu.SemaphoreType.DMA(())]
     here, there = pl.BlockSpec(memory_space=pltpu.VMEM), pl.BlockSpec(memory_space=pltpu.HBM)
@@ -331,7 +344,7 @@
         scratch_shapes=staged,
     )
     y, partly = call(
-        functools.partial(near_body, pairs),
+        functools.partial(near_body, stop, pairs),
         (y_shape, out),
         4 * pairs * one,
         queries,
@@ -348,24 +361,21 @@
         input_output_aliases={3: 1},
     )
     for pair in every:
-        partly = call(
-            functools.partial(last_body, pair),
-            out,
-            0,
-            own,
-            y,
-            partly,
-            *back[2 * pair : 2 * pair + 2],
-            in_specs=[here, here, there, here, here],
-            out_specs=there,
-            scratch_shapes=[pltpu.VMEM((rows, LANES), out.dtype), staged[1]],
-            input_output_aliases={2: 0},
-        )
+        for parity, came in back[pair]:
+            partly = call(
+                functools.partial(last_body, pair, parity),
+                out,
+                0,
+                own,
+                y,
+                partly,
+                came,
+                in_specs=[here, here, there, here],
+                out_specs=there,
+                scratch_shapes=[pltpu.VMEM((rows, LANES), out.dtype), staged[1]],
+                input_output_aliases={2: 0},
+            )
     return partly
-
-
-UP = "C"
-BACK = "CC"
 
 
 def solution(mesh):

time: 17.7 us -> 17.1 us (0.966)
  the two profiles are of different devices: /device:TPU:10 before, /device:TPU:13 now
where the time goes in v4:
time: 17.1 us; the launch traced here: 17 us
  starting transfers between devices  7.86 us (46%)
  waiting for transfers between devices  5.45 us (32%)
  Pallas kernels  3.55 us (21%)
    pallas_call x9, Pallas kernels, call(): pl.pallas_call(body, out_shape=out, cost_estimate=pl.CostEstimate(flops=f...  3.55 us
    ppermute x5, starting transfers between devices, trade(): lax.ppermute(x, 'ctx', [(i, i ^ 1) for i in range(lax.axis_size('ctx'))])  3.44 us
    ppermute x2, waiting for transfers between devices, snake(): return lax.ppermute(x, 'ctx', pairs)  3.04 us
    ppermute x2, starting transfers between devices, climb(): return lax.ppermute(x, 'ctx', pairs)  2.49 us
    ppermute x2, waiting for transfers between devices, exchange(): return lax.ppermute(x, 'ctx', pairs)  2.15 us
    ppermute x2, starting transfers between devices, snake(): return lax.ppermute(x, 'ctx', pairs)  1.48 us
    ppermute x2, starting transfers between devices, exchange(): return lax.ppermute(x, 'ctx', pairs)  0.45 us
  transfers between devices with their start and end apart: 11, of which 4 were waited for; matrix products, arithmetic and copies ran while one was open for 0% of the time, Pallas kernels for 15%

profile of v4, /device:TPU:13, one launch (start us, length us, event | category | flops | bytes accessed | tf_op | source)
XLA Modules:
  0.0 17.0 jit_solution(9037217627946498160)
XLA Ops:
  0.0 1.0 %shard_map.46 = (f32[264,128]{1,0:T(8,128)S(1)}, f32[264,128]{1,0:T(8,128)S(1)}, f32[256,128]{1,0:T(8,128)S(1)}, f32[1,128]{1,0:T(1,128)S(1)}) custom-call(bf16[128,256]{1,0:T(8,128)(2,1)} %k_hbm.1, bf16[128,256]{1,0:T(8,128)(2,1)} %v_hbm.1, bf16[128,256]{1,0:T(8,128)(2,1)} %q_ref.3, s32[1,128]{1,0:T(1,128)} %bitcast.1), custom_call_target="tpu_custom_call" | custom-call | bytes 197120 | tf_op jit(solution)/shard_map/pallas_call | solution.py:266
  1.0 1.3 %collective-permute-start.2 = (f32[264,128]{1,0:T(8,128)S(1)}, f32[264,128]{1,0:T(8,128)S(1)}, u32[]{:S(2)}, u32[]{:S(2)}) collective-permute-start(f32[264,128]{1,0:T(8,128)S(1)} %get-tuple-element.14.refs_0_), channel_id=1, source_target_pairs={{2,6},{0,2},{6,10},{4,0},{10,14},{8,4},{14,12},{12,8},{3,7},{1,3},... | collective-permute-start | bytes 405512 | tf_op jit(solution)/shard_map/ppermute | solution.py:26
  2.3 1.3 %collective-permute-start.3 = (f32[256,128]{1,0:T(8,128)S(1)}, f32[256,128]{1,0:T(8,128)S(1)}, u32[]{:S(2)}, u32[]{:S(2)}) collective-permute-start(f32[256,128]{1,0:T(8,128)S(1)} %get-tuple-element.15.refs_1_.refs_3_.mine), channel_id=1, source_target_pairs={{0,4},{2,6},{4,8},{6,10},{8,0},{10,2},{12,14},{14,12},{1,5},{3,7},... | collective-permute-start | bytes 393224 | tf_op jit(solution)/shard_map/ppermute | solution.py:36
  3.6 0.2 collective-permute-start.4
  3.8 0.0 collective-permute-start
  3.8 1.4 %collective-permute-done.2.refs_0_.high0.high = f32[264,128]{1,0:T(8,128)S(1)} collective-permute-done((f32[264,128]{1,0:T(8,128)S(1)}, f32[264,128]{1,0:T(8,128)S(1)}, u32[]{:S(2)}, u32[]{:S(2)}) %collective-permute-start.2) | collective-permute-done | bytes 135200 | tf_op jit(solution)/shard_map/ppermute | solution.py:26
  5.2 2.9 %collective-permute-start.5 = (f32[264,128]{1,0:T(8,128)S(1)}, f32[264,128]{1,0:T(8,128)S(1)}, u32[]{:S(2)}, u32[]{:S(2)}) collective-permute-start(f32[264,128]{1,0:T(8,128)S(1)} %collective-permute-done.2.refs_0_.high0.high), channel_id=1, source_target_pairs={{0,2},{2,0},{4,6},{6,4},{8,10},{10,8},{12,14},{14,12},{1,3},{3,1},... | collective-permute-start | bytes 405512 | tf_op jit(solution)/shard_map/ppermute | solution.py:51
  8.1 0.0 collective-permute-start.1
  8.1 0.0 collective-permute-done.3.refs_1_.refs_3_.high.low
  8.1 0.5 %collective-permute-start.6 = (f32[256,128]{1,0:T(8,128)S(1)}, f32[256,128]{1,0:T(8,128)S(1)}, u32[]{:S(2)}, u32[]{:S(2)}) collective-permute-start(f32[256,128]{1,0:T(8,128)S(1)} %collective-permute-done.3.refs_1_.refs_3_.high.low), channel_id=1, source_target_pairs={{0,2},{2,0},{4,6},{6,4},{8,10},{10,8},{12,14},{14,12},{1,3},{3,1},... | collective-permute-start | bytes 393224 | tf_op jit(solution)/shard_map/ppermute | solution.py:51
  8.6 1.7 %collective-permute-done.4.refs_2_.low0.low = f32[264,128]{1,0:T(8,128)S(1)} collective-permute-done((f32[264,128]{1,0:T(8,128)S(1)}, f32[264,128]{1,0:T(8,128)S(1)}, u32[]{:S(2)}, u32[]{:S(2)}) %collective-permute-start.4) | collective-permute-done | bytes 135200 | tf_op jit(solution)/shard_map/ppermute | solution.py:26
  10.2 0.0 collective-permute-start.7
  10.3 0.0 collective-permute-done.1.refs_5_.side
  10.3 0.0 collective-permute-done.refs_4_.side0
  10.3 0.0 collective-permute-done.5.refs_4_.side0.side
  10.3 0.3 %shard_map.49 = f32[128,128]{1,0:T(8,128)S(1)} custom-call(f32[264,128]{1,0:T(8,128)S(1)} %collective-permute-done.2.refs_0_.high0.high, f32[264,128]{1,0:T(8,128)S(1)} %collective-permute-done.4.refs_2_.low0.low, f32[264,128]{1,0:T(8,128)S(1)} %collective-permute-done.5.refs_4_.side0.side, f32[264,128]{1,0:T(8,128)S(1)} %collective-permute-done.2.refs_0_.high0.high, ...), custom_call_target="tpu_custom_call" | custom-call | flops 33554432 | bytes 811008 | tf_op jit(solution)/shard_map/pallas_call | solution.py:266
  10.7 0.0 copy-start
  10.7 1.2 %collective-permute-start.8 = (f32[128,128]{1,0:T(8,128)S(1)}, f32[128,128]{1,0:T(8,128)S(1)}, u32[]{:S(2)}, u32[]{:S(2)}) collective-permute-start(f32[128,128]{1,0:T(8,128)S(1)} %shard_map.49), channel_id=1, source_target_pairs={{0,2},{2,0},{4,8},{6,10},{8,12},{10,14},{12,4},{14,6},{1,3},{3,1},... | collective-permute-start | bytes 196616 | tf_op jit(solution)/shard_map/ppermute | solution.py:36
  11.9 0.0 collective-permute-done.6.refs_5_.refs_7_.side
  11.9 0.3 %shard_map.52 = f32[128,128]{1,0:T(8,128)S(1)} custom-call(f32[264,128]{1,0:T(8,128)S(1)} %collective-permute-done.2.refs_0_.high0.high, f32[264,128]{1,0:T(8,128)S(1)} %collective-permute-done.4.refs_2_.low0.low, f32[264,128]{1,0:T(8,128)S(1)} %collective-permute-done.5.refs_4_.side0.side, f32[256,128]{1,0:T(8,128)S(1)} %collective-permute-done.3.refs_1_.refs_3_.high.low, ...), custom_call_target="tpu_custom_call" | custom-call | flops 33554432 | bytes 864256 | tf_op jit(solution)/shard_map/pallas_call | solution.py:266
  12.2 0.1 collective-permute-start.9
  12.3 0.3 %collective-permute-start.10 = (f32[128,128]{1,0:T(8,128)S(1)}, f32[128,128]{1,0:T(8,128)S(1)}, u32[]{:S(2)}, u32[]{:S(2)}) collective-permute-start(f32[128,128]{1,0:T(8,128)S(1)} %shard_map.52), channel_id=1, source_target_pairs={{0,2},{2,0},{4,6},{6,4},{8,12},{10,14},{12,8},{14,10},{1,3},{3,1},... | collective-permute-start | bytes 196616 | tf_op jit(solution)/shard_map/ppermute | solution.py:47
  12.6 0.0 copy-done
  12.6 0.5 %shard_map.47 = (f32[256,128]{1,0:T(8,128)S(1)}, bf16[128,256]{1,0:T(8,128)(2,1)}) custom-call(bf16[128,256]{1,0:T(8,128)(2,1)S(1)} %copy-done, f32[264,128]{1,0:T(8,128)S(1)} %get-tuple-element.14.refs_0_, f32[256,128]{1,0:T(8,128)S(1)} %get-tuple-element.15.refs_1_.refs_3_.mine, f32[264,128]{1,0:T(8,128)S(1)} %get-tuple-element.16.refs_2_, ...), custom_call_target="tpu_custom_call" | custom-call | flops 67108864 | bytes 864256 | tf_op jit(solution)/shard_map/pallas_call | solution.py:266
  13.1 0.0 collective-permute-done.7.refs_6_
  13.2 1.3 %shard_map.48 = (f32[256,128]{1,0:T(8,128)S(1)}, bf16[128,256]{1,0:T(8,128)(2,1)}) custom-call(bf16[128,256]{1,0:T(8,128)(2,1)S(1)} %copy-done, f32[1,128]{1,0:T(1,128)S(1)} %get-tuple-element.13.own_ref, f32[256,128]{1,0:T(8,128)S(1)} %get-tuple-element.17.y_ref, bf16[128,256]{1,0:T(8,128)(2,1)} %get-tuple-element.18._, ...), custom_call_target="tpu_custom_call", output_to_operand_aliasing={{1}: (3, {})} | custom-call | flops 67108864 | bytes 1327616 | tf_op jit(solution)/shard_map/pallas_call | solution.py:266
  14.5 0.2 %collective-permute-done.8.came = f32[128,128]{1,0:T(8,128)S(1)} collective-permute-done((f32[128,128]{1,0:T(8,128)S(1)}, f32[128,128]{1,0:T(8,128)S(1)}, u32[]{:S(2)}, u32[]{:S(2)}) %collective-permute-start.8) | collective-permute-done | bytes 65568 | tf_op jit(solution)/shard_map/ppermute | solution.py:36
  14.7 2.1 %collective-permute-done.9.came = f32[128,128]{1,0:T(8,128)S(1)} collective-permute-done((f32[128,128]{1,0:T(8,128)S(1)}, f32[128,128]{1,0:T(8,128)S(1)}, u32[]{:S(2)}, u32[]{:S(2)}) %collective-permute-start.9) | collective-permute-done | bytes 65568 | tf_op jit(solution)/shard_map/ppermute | solution.py:47
  16.9 0.0 collective-permute-done.10.came
  (4 shorter events, 0.1 us)
Async XLA Ops:
  1.0 4.2 %collective-permute-start.2 = (f32[264,128]{1,0:T(8,128)S(1)}, f32[264,128]{1,0:T(8,128)S(1)}, u32[]{:S(2)}, u32[]{:S(2)}) collective-permute-start(f32[264,128]{1,0:T(8,128)S(1)} %get-tuple-element.14.refs_0_), channel_id=1, source_target_pairs={{2,6},{0,2},{6,10},{4,0},{10,14},{8,4},{14,12},{12,8},{3,7},{1,3},... | collective-permute-start | bytes 405512 | tf_op jit(solution)/shard_map/ppermute | solution.py:26
  2.3 5.8 %collective-permute-start.3 = (f32[256,128]{1,0:T(8,128)S(1)}, f32[256,128]{1,0:T(8,128)S(1)}, u32[]{:S(2)}, u32[]{:S(2)}) collective-permute-start(f32[256,128]{1,0:T(8,128)S(1)} %get-tuple-element.15.refs_1_.refs_3_.mine), channel_id=1, source_target_pairs={{0,4},{2,6},{4,8},{6,10},{8,0},{10,2},{12,14},{14,12},{1,5},{3,7},... | collective-permute-start | bytes 393224 | tf_op jit(solution)/shard_map/ppermute | solution.py:36
  3.6 6.7 %collective-permute-start.4 = (f32[264,128]{1,0:T(8,128)S(1)}, f32[264,128]{1,0:T(8,128)S(1)}, u32[]{:S(2)}, u32[]{:S(2)}) collective-permute-start(f32[264,128]{1,0:T(8,128)S(1)} %get-tuple-element.16.refs_2_), channel_id=1, source_target_pairs={{0,4},{2,0},{4,8},{6,2},{8,12},{10,6},{12,14},{14,10},{1,5},{3,1},... | collective-permute-start | bytes 405512 | tf_op jit(solution)/shard_map/ppermute | solution.py:26
  3.8 6.5 %collective-permute-start = (f32[264,128]{1,0:T(8,128)S(1)}, f32[264,128]{1,0:T(8,128)S(1)}, u32[]{:S(2)}, u32[]{:S(2)}) collective-permute-start(f32[264,128]{1,0:T(8,128)S(1)} %get-tuple-element.16.refs_2_), channel_id=1, source_target_pairs={{0,2},{2,0},{4,6},{6,4},{8,10},{10,8},{12,14},{14,12},{1,3},{3,1},... | collective-permute-start | bytes 405512 | tf_op jit(solution)/shard_map/ppermute | solution.py:51
  5.2 5.1 %collective-permute-start.5 = (f32[264,128]{1,0:T(8,128)S(1)}, f32[264,128]{1,0:T(8,128)S(1)}, u32[]{:S(2)}, u32[]{:S(2)}) collective-permute-start(f32[264,128]{1,0:T(8,128)S(1)} %collective-permute-done.2.refs_0_.high0.high), channel_id=1, source_target_pairs={{0,2},{2,0},{4,6},{6,4},{8,10},{10,8},{12,14},{14,12},{1,3},{3,1},... | collective-permute-start | bytes 405512 | tf_op jit(solution)/shard_map/ppermute | solution.py:51
  8.1 2.2 %collective-permute-start.1 = (f32[256,128]{1,0:T(8,128)S(1)}, f32[256,128]{1,0:T(8,128)S(1)}, u32[]{:S(2)}, u32[]{:S(2)}) collective-permute-start(f32[256,128]{1,0:T(8,128)S(1)} %get-tuple-element.15.refs_1_.refs_3_.mine), channel_id=1, source_target_pairs={{0,2},{2,0},{4,6},{6,4},{8,10},{10,8},{12,14},{14,12},{1,3},{3,1},... | collective-permute-start | bytes 393224 | tf_op jit(solution)/shard_map/ppermute | solution.py:51
  8.1 3.8 %collective-permute-start.6 = (f32[256,128]{1,0:T(8,128)S(1)}, f32[256,128]{1,0:T(8,128)S(1)}, u32[]{:S(2)}, u32[]{:S(2)}) collective-permute-start(f32[256,128]{1,0:T(8,128)S(1)} %collective-permute-done.3.refs_1_.refs_3_.high.low), channel_id=1, source_target_pairs={{0,2},{2,0},{4,6},{6,4},{8,10},{10,8},{12,14},{14,12},{1,3},{3,1},... | collective-permute-start | bytes 393224 | tf_op jit(solution)/shard_map/ppermute | solution.py:51
  10.2 2.9 %collective-permute-start.7 = (f32[264,128]{1,0:T(8,128)S(1)}, f32[264,128]{1,0:T(8,128)S(1)}, u32[]{:S(2)}, u32[]{:S(2)}) collective-permute-start(f32[264,128]{1,0:T(8,128)S(1)} %collective-permute-done.4.refs_2_.low0.low), channel_id=1, source_target_pairs={{0,2},{2,0},{4,6},{6,4},{8,10},{10,8},{12,14},{14,12},{1,3},{3,1},... | collective-permute-start | bytes 405512 | tf_op jit(solution)/shard_map/ppermute | solution.py:51
  10.7 2.0 %copy-start = (bf16[128,256]{1,0:T(8,128)(2,1)S(1)}, bf16[128,256]{1,0:T(8,128)(2,1)}, u32[]{:S(2)}) copy-start(bf16[128,256]{1,0:T(8,128)(2,1)} %q_ref.3) | copy-start | bytes 196612
  10.7 4.1 %collective-permute-start.8 = (f32[128,128]{1,0:T(8,128)S(1)}, f32[128,128]{1,0:T(8,128)S(1)}, u32[]{:S(2)}, u32[]{:S(2)}) collective-permute-start(f32[128,128]{1,0:T(8,128)S(1)} %shard_map.49), channel_id=1, source_target_pairs={{0,2},{2,0},{4,8},{6,10},{8,12},{10,14},{12,4},{14,6},{1,3},{3,1},... | collective-permute-start | bytes 196616 | tf_op jit(solution)/shard_map/ppermute | solution.py:36
  12.2 4.7 %collective-permute-start.9 = (f32[128,128]{1,0:T(8,128)S(1)}, f32[128,128]{1,0:T(8,128)S(1)}, u32[]{:S(2)}, u32[]{:S(2)}) collective-permute-start(f32[128,128]{1,0:T(8,128)S(1)} %shard_map.52), channel_id=1, source_target_pairs={{0,2},{2,0},{4,8},{6,10},{8,4},{10,6},{12,14},{14,12},{1,3},{3,1},... | collective-permute-start | bytes 196616 | tf_op jit(solution)/shard_map/ppermute | solution.py:47
  12.3 4.6 %collective-permute-start.10 = (f32[128,128]{1,0:T(8,128)S(1)}, f32[128,128]{1,0:T(8,128)S(1)}, u32[]{:S(2)}, u32[]{:S(2)}) collective-permute-start(f32[128,128]{1,0:T(8,128)S(1)} %shard_map.52), channel_id=1, source_target_pairs={{0,2},{2,0},{4,6},{6,4},{8,12},{10,14},{12,8},{14,10},{1,3},{3,1},... | collective-permute-start | bytes 196616 | tf_op jit(solution)/shard_map/ppermute | solution.py:47

commit v5 on v4

--- a/solution.py
+++ b/solution.py
@@ -110,37 +110,46 @@
     for at, (source, target) in enumerate(routes):
         moves.append(pltpu.make_async_copy(source, target, sem.at[at]))
         moves[-1].start()
-    for item in moves:
-        item.wait()
+    odd = is_odd()
+    size = high.shape[0] - TILE
+
+    def each_side(put):
+        @pl.when(odd)
+        def _():
+            put(high, low)
+
+        @pl.when(jnp.logical_not(odd))
+        def _():
+            put(low, high)
+
+    moves[0].wait()
+    moves[1].wait()
+
+    def put_up(up, _):
+        up[:rows, :] = k_ref[:, cut(0)].astype(jnp.float32)
+        up[rows : 2 * rows, :] = v_ref[:, cut(0)].astype(jnp.float32)
+        if 2 * rows < size:
+            up[2 * rows : size, :] = jnp.zeros((size - 2 * rows, LANES), jnp.float32)
+
+    each_side(put_up)
+    for pair in range(1, pairs):
+        rest[pair - 1][:rows, :] = k_ref[:, cut(pair)].astype(jnp.float32)
+        rest[pair - 1][rows : 2 * rows, :] = v_ref[:, cut(pair)].astype(jnp.float32)
+    moves[2].wait()
+
+    def put_down(_, down):
+        for pair in range(pairs):
+            down[pair * rows : (pair + 1) * rows, :] = q_ref[:, cut(pair)].astype(jnp.float32)
+        if pairs * rows < size:
+            down[pairs * rows : size, :] = jnp.zeros((size - pairs * rows, LANES), jnp.float32)
+
+    each_side(put_down)
+    moves[3].wait()
     ids = ids_ref[...].astype(jnp.float32)
     own_ref[...] = ids
     wide = jnp.broadcast_to(ids, (TILE, rows))
-    odd = is_odd()
-
-    def put(target, pair):
-        target[:rows, :] = k_ref[:, cut(pair)].astype(jnp.float32)
-        target[rows : 2 * rows, :] = v_ref[:, cut(pair)].astype(jnp.float32)
-
-    def fill(up, down):
-        size = up.shape[0] - TILE
-        put(up, 0)
-        for pair in range(pairs):
-            down[pair * rows : (pair + 1) * rows, :] = q_ref[:, cut(pair)].astype(jnp.float32)
-        for target, done in ((up, 2 * rows), (down, pairs * rows)):
-            if done < size:
-                target[done:size, :] = jnp.zeros((size - done, LANES), jnp.float32)
-            target[size:, :] = wide
-
-    @pl.when(odd)
-    def _():
-        fill(high, low)
-
-    @pl.when(jnp.logical_not(odd))
-    def _():
-        fill(low, high)
-
-    for pair in range(1, pairs):
-        put(rest[pair - 1], pair)
+    high[size:, :] = wide
+    low[size:, :] = wide
 
 
 def local_body(pairs, q_ref, *refs):

time: 17.1 us -> 17.1 us (level)
  no operation moved by 1% of the time
where the time goes in v5:
time: 17.1 us; the launch traced here: 16.9 us
  starting transfers between devices  7.86 us (46%)
  waiting for transfers between devices  5.46 us (32%)
  Pallas kernels  3.53 us (21%)
    pallas_call x9, Pallas kernels, call(): pl.pallas_call(body, out_shape=out, cost_estimate=pl.CostEstimate(flops=f...  3.53 us
    ppermute x5, starting transfers between devices, trade(): lax.ppermute(x, 'ctx', [(i, i ^ 1) for i in range(lax.axis_size('ctx'))])  3.45 us
    ppermute x2, waiting for transfers between devices, snake(): return lax.ppermute(x, 'ctx', pairs)  3.04 us
    ppermute x2, starting transfers between devices, climb(): return lax.ppermute(x, 'ctx', pairs)  2.49 us
    ppermute x2, waiting for transfers between devices, exchange(): return lax.ppermute(x, 'ctx', pairs)  2.15 us
    ppermute x2, starting transfers between devices, snake(): return lax.ppermute(x, 'ctx', pairs)  1.48 us
    ppermute x2, starting transfers between devices, exchange(): return lax.ppermute(x, 'ctx', pairs)  0.44 us
  transfers between devices with their start and end apart: 11, of which 4 were waited for; matrix products, arithmetic and copies ran while one was open for 0% of the time, Pallas kernels for 15%

profile of v5, /device:TPU:13, one launch (start us, length us, event | category | flops | bytes accessed | tf_op | source)
XLA Modules:
  0.0 16.9 jit_solution(3110191338077597523)
XLA Ops:
  0.0 0.9 %shard_map.46 = (f32[264,128]{1,0:T(8,128)S(1)}, f32[264,128]{1,0:T(8,128)S(1)}, f32[256,128]{1,0:T(8,128)S(1)}, f32[1,128]{1,0:T(1,128)S(1)}) custom-call(bf16[128,256]{1,0:T(8,128)(2,1)} %k_hbm.1, bf16[128,256]{1,0:T(8,128)(2,1)} %v_hbm.1, bf16[128,256]{1,0:T(8,128)(2,1)} %q_ref.3, s32[1,128]{1,0:T(1,128)} %bitcast.1), custom_call_target="tpu_custom_call" | custom-call | bytes 197120 | tf_op jit(solution)/shard_map/pallas_call | solution.py:275
  1.0 1.3 %collective-permute-start.2 = (f32[264,128]{1,0:T(8,128)S(1)}, f32[264,128]{1,0:T(8,128)S(1)}, u32[]{:S(2)}, u32[]{:S(2)}) collective-permute-start(f32[264,128]{1,0:T(8,128)S(1)} %get-tuple-element.14.refs_0_), channel_id=1, source_target_pairs={{2,6},{0,2},{6,10},{4,0},{10,14},{8,4},{14,12},{12,8},{3,7},{1,3},... | collective-permute-start | bytes 405512 | tf_op jit(solution)/shard_map/ppermute | solution.py:26
  2.3 1.3 %collective-permute-start.3 = (f32[256,128]{1,0:T(8,128)S(1)}, f32[256,128]{1,0:T(8,128)S(1)}, u32[]{:S(2)}, u32[]{:S(2)}) collective-permute-start(f32[256,128]{1,0:T(8,128)S(1)} %get-tuple-element.15.refs_1_.refs_3_.mine), channel_id=1, source_target_pairs={{0,4},{2,6},{4,8},{6,10},{8,0},{10,2},{12,14},{14,12},{1,5},{3,7},... | collective-permute-start | bytes 393224 | tf_op jit(solution)/shard_map/ppermute | solution.py:36
  3.6 0.2 %collective-permute-start.4 = (f32[264,128]{1,0:T(8,128)S(1)}, f32[264,128]{1,0:T(8,128)S(1)}, u32[]{:S(2)}, u32[]{:S(2)}) collective-permute-start(f32[264,128]{1,0:T(8,128)S(1)} %get-tuple-element.16.refs_2_), channel_id=1, source_target_pairs={{0,4},{2,0},{4,8},{6,2},{8,12},{10,6},{12,14},{14,10},{1,5},{3,1},... | collective-permute-start | bytes 405512 | tf_op jit(solution)/shard_map/ppermute | solution.py:26
  3.7 0.0 collective-permute-start
  3.7 1.4 %collective-permute-done.2.refs_0_.high0.high = f32[264,128]{1,0:T(8,128)S(1)} collective-permute-done((f32[264,128]{1,0:T(8,128)S(1)}, f32[264,128]{1,0:T(8,128)S(1)}, u32[]{:S(2)}, u32[]{:S(2)}) %collective-permute-start.2) | collective-permute-done | bytes 135200 | tf_op jit(solution)/shard_map/ppermute | solution.py:26
  5.1 2.9 %collective-permute-start.5 = (f32[264,128]{1,0:T(8,128)S(1)}, f32[264,128]{1,0:T(8,128)S(1)}, u32[]{:S(2)}, u32[]{:S(2)}) collective-permute-start(f32[264,128]{1,0:T(8,128)S(1)} %collective-permute-done.2.refs_0_.high0.high), channel_id=1, source_target_pairs={{0,2},{2,0},{4,6},{6,4},{8,10},{10,8},{12,14},{14,12},{1,3},{3,1},... | collective-permute-start | bytes 405512 | tf_op jit(solution)/shard_map/ppermute | solution.py:51
  8.1 0.0 collective-permute-start.1
  8.1 0.0 collective-permute-done.3.refs_1_.refs_3_.high.low
  8.1 0.5 %collective-permute-start.6 = (f32[256,128]{1,0:T(8,128)S(1)}, f32[256,128]{1,0:T(8,128)S(1)}, u32[]{:S(2)}, u32[]{:S(2)}) collective-permute-start(f32[256,128]{1,0:T(8,128)S(1)} %collective-permute-done.3.refs_1_.refs_3_.high.low), channel_id=1, source_target_pairs={{0,2},{2,0},{4,6},{6,4},{8,10},{10,8},{12,14},{14,12},{1,3},{3,1},... | collective-permute-start | bytes 393224 | tf_op jit(solution)/shard_map/ppermute | solution.py:51
  8.6 1.7 %collective-permute-done.4.refs_2_.low0.low = f32[264,128]{1,0:T(8,128)S(1)} collective-permute-done((f32[264,128]{1,0:T(8,128)S(1)}, f32[264,128]{1,0:T(8,128)S(1)}, u32[]{:S(2)}, u32[]{:S(2)}) %collective-permute-start.4) | collective-permute-done | bytes 135200 | tf_op jit(solution)/shard_map/ppermute | solution.py:26
  10.2 0.0 collective-permute-start.7
  10.2 0.0 collective-permute-done.1.refs_5_.side
  10.2 0.0 collective-permute-done.refs_4_.side0
  10.3 0.0 collective-permute-done.5.refs_4_.side0.side
  10.3 0.3 %shard_map.49 = f32[128,128]{1,0:T(8,128)S(1)} custom-call(f32[264,128]{1,0:T(8,128)S(1)} %collective-permute-done.2.refs_0_.high0.high, f32[264,128]{1,0:T(8,128)S(1)} %collective-permute-done.4.refs_2_.low0.low, f32[264,128]{1,0:T(8,128)S(1)} %collective-permute-done.5.refs_4_.side0.side, f32[264,128]{1,0:T(8,128)S(1)} %collective-permute-done.2.refs_0_.high0.high, ...), custom_call_target="tpu_custom_call" | custom-call | flops 33554432 | bytes 811008 | tf_op jit(solution)/shard_map/pallas_call | solution.py:275
  10.6 0.0 copy-start
  10.6 1.2 %collective-permute-start.8 = (f32[128,128]{1,0:T(8,128)S(1)}, f32[128,128]{1,0:T(8,128)S(1)}, u32[]{:S(2)}, u32[]{:S(2)}) collective-permute-start(f32[128,128]{1,0:T(8,128)S(1)} %shard_map.49), channel_id=1, source_target_pairs={{0,2},{2,0},{4,8},{6,10},{8,12},{10,14},{12,4},{14,6},{1,3},{3,1},... | collective-permute-start | bytes 196616 | tf_op jit(solution)/shard_map/ppermute | solution.py:36
  11.8 0.0 collective-permute-done.6.refs_5_.refs_7_.side
  11.8 0.3 %shard_map.52 = f32[128,128]{1,0:T(8,128)S(1)} custom-call(f32[264,128]{1,0:T(8,128)S(1)} %collective-permute-done.2.refs_0_.high0.high, f32[264,128]{1,0:T(8,128)S(1)} %collective-permute-done.4.refs_2_.low0.low, f32[264,128]{1,0:T(8,128)S(1)} %collective-permute-done.5.refs_4_.side0.side, f32[256,128]{1,0:T(8,128)S(1)} %collective-permute-done.3.refs_1_.refs_3_.high.low, ...), custom_call_target="tpu_custom_call" | custom-call | flops 33554432 | bytes 864256 | tf_op jit(solution)/shard_map/pallas_call | solution.py:275
  12.2 0.1 collective-permute-start.9
  12.3 0.3 %collective-permute-start.10 = (f32[128,128]{1,0:T(8,128)S(1)}, f32[128,128]{1,0:T(8,128)S(1)}, u32[]{:S(2)}, u32[]{:S(2)}) collective-permute-start(f32[128,128]{1,0:T(8,128)S(1)} %shard_map.52), channel_id=1, source_target_pairs={{0,2},{2,0},{4,6},{6,4},{8,12},{10,14},{12,8},{14,10},{1,3},{3,1},... | collective-permute-start | bytes 196616 | tf_op jit(solution)/shard_map/ppermute | solution.py:47
  12.6 0.0 copy-done
  12.6 0.5 %shard_map.47 = (f32[256,128]{1,0:T(8,128)S(1)}, bf16[128,256]{1,0:T(8,128)(2,1)}) custom-call(bf16[128,256]{1,0:T(8,128)(2,1)S(1)} %copy-done, f32[264,128]{1,0:T(8,128)S(1)} %get-tuple-element.14.refs_0_, f32[256,128]{1,0:T(8,128)S(1)} %get-tuple-element.15.refs_1_.refs_3_.mine, f32[264,128]{1,0:T(8,128)S(1)} %get-tuple-element.16.refs_2_, ...), custom_call_target="tpu_custom_call" | custom-call | flops 67108864 | bytes 864256 | tf_op jit(solution)/shard_map/pallas_call | solution.py:275
  13.1 0.0 collective-permute-done.7.refs_6_
  13.1 1.3 %shard_map.48 = (f32[256,128]{1,0:T(8,128)S(1)}, bf16[128,256]{1,0:T(8,128)(2,1)}) custom-call(bf16[128,256]{1,0:T(8,128)(2,1)S(1)} %copy-done, f32[1,128]{1,0:T(1,128)S(1)} %get-tuple-element.13.own_ref, f32[256,128]{1,0:T(8,128)S(1)} %get-tuple-element.17.y_ref, bf16[128,256]{1,0:T(8,128)(2,1)} %get-tuple-element.18._, ...), custom_call_target="tpu_custom_call", output_to_operand_aliasing={{1}: (3, {})} | custom-call | flops 67108864 | bytes 1327616 | tf_op jit(solution)/shard_map/pallas_call | solution.py:275
  14.5 0.2 %collective-permute-done.8.came = f32[128,128]{1,0:T(8,128)S(1)} collective-permute-done((f32[128,128]{1,0:T(8,128)S(1)}, f32[128,128]{1,0:T(8,128)S(1)}, u32[]{:S(2)}, u32[]{:S(2)}) %collective-permute-start.8) | collective-permute-done | bytes 65568 | tf_op jit(solution)/shard_map/ppermute | solution.py:36
  14.7 2.1 %collective-permute-done.9.came = f32[128,128]{1,0:T(8,128)S(1)} collective-permute-done((f32[128,128]{1,0:T(8,128)S(1)}, f32[128,128]{1,0:T(8,128)S(1)}, u32[]{:S(2)}, u32[]{:S(2)}) %collective-permute-start.9) | collective-permute-done | bytes 65568 | tf_op jit(solution)/shard_map/ppermute | solution.py:47
  16.9 0.0 collective-permute-done.10.came
  (4 shorter events, 0.1 us)
Async XLA Ops:
  1.0 4.2 %collective-permute-start.2 = (f32[264,128]{1,0:T(8,128)S(1)}, f32[264,128]{1,0:T(8,128)S(1)}, u32[]{:S(2)}, u32[]{:S(2)}) collective-permute-start(f32[264,128]{1,0:T(8,128)S(1)} %get-tuple-element.14.refs_0_), channel_id=1, source_target_pairs={{2,6},{0,2},{6,10},{4,0},{10,14},{8,4},{14,12},{12,8},{3,7},{1,3},... | collective-permute-start | bytes 405512 | tf_op jit(solution)/shard_map/ppermute | solution.py:26
  2.3 5.8 %collective-permute-start.3 = (f32[256,128]{1,0:T(8,128)S(1)}, f32[256,128]{1,0:T(8,128)S(1)}, u32[]{:S(2)}, u32[]{:S(2)}) collective-permute-start(f32[256,128]{1,0:T(8,128)S(1)} %get-tuple-element.15.refs_1_.refs_3_.mine), channel_id=1, source_target_pairs={{0,4},{2,6},{4,8},{6,10},{8,0},{10,2},{12,14},{14,12},{1,5},{3,7},... | collective-permute-start | bytes 393224 | tf_op jit(solution)/shard_map/ppermute | solution.py:36
  3.6 6.7 %collective-permute-start.4 = (f32[264,128]{1,0:T(8,128)S(1)}, f32[264,128]{1,0:T(8,128)S(1)}, u32[]{:S(2)}, u32[]{:S(2)}) collective-permute-start(f32[264,128]{1,0:T(8,128)S(1)} %get-tuple-element.16.refs_2_), channel_id=1, source_target_pairs={{0,4},{2,0},{4,8},{6,2},{8,12},{10,6},{12,14},{14,10},{1,5},{3,1},... | collective-permute-start | bytes 405512 | tf_op jit(solution)/shard_map/ppermute | solution.py:26
  3.7 6.5 %collective-permute-start = (f32[264,128]{1,0:T(8,128)S(1)}, f32[264,128]{1,0:T(8,128)S(1)}, u32[]{:S(2)}, u32[]{:S(2)}) collective-permute-start(f32[264,128]{1,0:T(8,128)S(1)} %get-tuple-element.16.refs_2_), channel_id=1, source_target_pairs={{0,2},{2,0},{4,6},{6,4},{8,10},{10,8},{12,14},{14,12},{1,3},{3,1},... | collective-permute-start | bytes 405512 | tf_op jit(solution)/shard_map/ppermute | solution.py:51
  5.1 5.1 %collective-permute-start.5 = (f32[264,128]{1,0:T(8,128)S(1)}, f32[264,128]{1,0:T(8,128)S(1)}, u32[]{:S(2)}, u32[]{:S(2)}) collective-permute-start(f32[264,128]{1,0:T(8,128)S(1)} %collective-permute-done.2.refs_0_.high0.high), channel_id=1, source_target_pairs={{0,2},{2,0},{4,6},{6,4},{8,10},{10,8},{12,14},{14,12},{1,3},{3,1},... | collective-permute-start | bytes 405512 | tf_op jit(solution)/shard_map/ppermute | solution.py:51
  8.1 2.2 %collective-permute-start.1 = (f32[256,128]{1,0:T(8,128)S(1)}, f32[256,128]{1,0:T(8,128)S(1)}, u32[]{:S(2)}, u32[]{:S(2)}) collective-permute-start(f32[256,128]{1,0:T(8,128)S(1)} %get-tuple-element.15.refs_1_.refs_3_.mine), channel_id=1, source_target_pairs={{0,2},{2,0},{4,6},{6,4},{8,10},{10,8},{12,14},{14,12},{1,3},{3,1},... | collective-permute-start | bytes 393224 | tf_op jit(solution)/shard_map/ppermute | solution.py:51
  8.1 3.8 %collective-permute-start.6 = (f32[256,128]{1,0:T(8,128)S(1)}, f32[256,128]{1,0:T(8,128)S(1)}, u32[]{:S(2)}, u32[]{:S(2)}) collective-permute-start(f32[256,128]{1,0:T(8,128)S(1)} %collective-permute-done.3.refs_1_.refs_3_.high.low), channel_id=1, source_target_pairs={{0,2},{2,0},{4,6},{6,4},{8,10},{10,8},{12,14},{14,12},{1,3},{3,1},... | collective-permute-start | bytes 393224 | tf_op jit(solution)/shard_map/ppermute | solution.py:51
  10.2 2.9 %collective-permute-start.7 = (f32[264,128]{1,0:T(8,128)S(1)}, f32[264,128]{1,0:T(8,128)S(1)}, u32[]{:S(2)}, u32[]{:S(2)}) collective-permute-start(f32[264,128]{1,0:T(8,128)S(1)} %collective-permute-done.4.refs_2_.low0.low), channel_id=1, source_target_pairs={{0,2},{2,0},{4,6},{6,4},{8,10},{10,8},{12,14},{14,12},{1,3},{3,1},... | collective-permute-start | bytes 405512 | tf_op jit(solution)/shard_map/ppermute | solution.py:51
  10.6 2.0 %copy-start = (bf16[128,256]{1,0:T(8,128)(2,1)S(1)}, bf16[128,256]{1,0:T(8,128)(2,1)}, u32[]{:S(2)}) copy-start(bf16[128,256]{1,0:T(8,128)(2,1)} %q_ref.3) | copy-start | bytes 196612
  10.6 4.1 %collective-permute-start.8 = (f32[128,128]{1,0:T(8,128)S(1)}, f32[128,128]{1,0:T(8,128)S(1)}, u32[]{:S(2)}, u32[]{:S(2)}) collective-permute-start(f32[128,128]{1,0:T(8,128)S(1)} %shard_map.49), channel_id=1, source_target_pairs={{0,2},{2,0},{4,8},{6,10},{8,12},{10,14},{12,4},{14,6},{1,3},{3,1},... | collective-permute-start | bytes 196616 | tf_op jit(solution)/shard_map/ppermute | solution.py:36
  12.2 4.7 %collective-permute-start.9 = (f32[128,128]{1,0:T(8,128)S(1)}, f32[128,128]{1,0:T(8,128)S(1)}, u32[]{:S(2)}, u32[]{:S(2)}) collective-permute-start(f32[128,128]{1,0:T(8,128)S(1)} %shard_map.52), channel_id=1, source_target_pairs={{0,2},{2,0},{4,8},{6,10},{8,4},{10,6},{12,14},{14,12},{1,3},{3,1},... | collective-permute-start | bytes 196616 | tf_op jit(solution)/shard_map/ppermute | solution.py:47
  12.3 4.6 %collective-permute-start.10 = (f32[128,128]{1,0:T(8,128)S(1)}, f32[128,128]{1,0:T(8,128)S(1)}, u32[]{:S(2)}, u32[]{:S(2)}) collective-permute-start(f32[128,128]{1,0:T(8,128)S(1)} %shard_map.52), channel_id=1, source_target_pairs={{0,2},{2,0},{4,6},{6,4},{8,12},{10,14},{12,8},{14,10},{1,3},{3,1},... | collective-permute-start | bytes 196616 | tf_op jit(solution)/shard_map/ppermute | solution.py:47

commit v6 on v4

--- a/solution.py
+++ b/solution.py
@@ -16,13 +16,13 @@
 GRANT = 16 << 20
 
 
-def snake(x, rising):
+def snake(x, rising, first):
     couples = lax.axis_size("ctx") // 2
     pairs = []
     for couple in range(couples):
         up, down = 2 * couple + rising, 2 * couple + 1 - rising
-        pairs.append((up, up + 2 if couple < couples - 1 else down))
-        pairs.append((down, down - 2 if couple > 0 else up))
+        pairs.append((up, up + 2 if first <= couple < couples - 1 else down))
+        pairs.append((down, down - 2 if couple > first else up))
     return lax.ppermute(x, "ctx", pairs)
 
 
@@ -59,20 +59,22 @@
     return lax.broadcasted_iota(jnp.int32, shape, 1) % LANES < HW
 
 
-def two_heads(block):
-    low = lower_half(block.shape)
-    zero = jnp.zeros_like(block)
-    both = jnp.concatenate([jnp.where(low, block, zero), jnp.where(low, zero, block)], axis=0)
-    return both.astype(jnp.bfloat16)
-
-
-def attend(q_two, keys, values, mask):
+def attend(q_two, blocks):
+    rows = q_two.shape[0]
+    low = lower_half(q_two.shape)
+    zero = jnp.zeros_like(q_two)
+    stacked = jnp.concatenate([jnp.where(low, q_two, zero), jnp.where(low, zero, q_two)], axis=0)
+    keys = jnp.concatenate([block[0].astype(jnp.bfloat16) for block in blocks], axis=0)
+    values = jnp.concatenate([block[1].astype(jnp.bfloat16) for block in blocks], axis=0)
+    masks = [jnp.broadcast_to(mask, (rows, mask.shape[1])) for _, _, mask in blocks]
+    mask = jnp.concatenate(masks, axis=1)
+    mask = jnp.concatenate([mask, mask], axis=0)
     scores = lax.dot_general(
-        q_two, two_heads(keys), (((1,), (1,)), ((), ())), preferred_element_type=jnp.float32
+        stacked, keys, (((1,), (1,)), ((), ())), preferred_element_type=jnp.float32
     )
-    mask = jnp.concatenate([mask, mask], axis=1)
     weights = jnp.where(mask, scores * scores, jnp.zeros_like(scores)).astype(jnp.bfloat16)
-    return jnp.dot(weights, two_heads(values), preferred_element_type=jnp.float32)
+    both = jnp.dot(weights, values, preferred_element_type=jnp.float32)
+    return jnp.where(low, both[:rows, :], both[rows:, :])
 
 
 def pick(flag, this, other, start, size):
@@ -156,9 +158,9 @@
     before = jnp.where(odd, pick_ids(odd, side[0], side[0]), -1.0) == ids[:, 0:1]
     for pair in range(pairs):
         q_two = q_ref[:, cut(pair)]
-        near = attend(q_two, *pick_pair(odd, high, low, pair, rows), allowed)
-        earlier = attend(q_two, *pick_pair(odd, side, side, pair, rows), before)
-        y_ref[pair * rows : (pair + 1) * rows, :] = near + jnp.where(seen, earlier, 0.0)
+        mine = (*pick_pair(odd, high, low, pair, rows), allowed)
+        earlier = (*pick_pair(odd, side, side, pair, rows), before & seen)
+        y_ref[pair * rows : (pair + 1) * rows, :] = attend(q_two, [mine, earlier])
     deliver_if(lax.axis_index("ctx") < 2, pairs, y_ref, o_hbm, o_ref, sem)
 
 
@@ -201,10 +203,11 @@
         below = lax.axis_index("ctx") < 2 * stop
         for pair in range(pairs):
             q_two = q_ref[:, cut(pair)]
-            total = jnp.zeros((rows, LANES), jnp.float32)
+            blocks = []
             for (this, other), mask in zip(sources, masks, strict=True):
                 mask = mask if pair == 0 else mask & below
-                total = total + attend(q_two, *pick_pair(odd, this, other, pair, rows), mask)
+                blocks.append((*pick_pair(odd, this, other, pair, rows), mask))
+            total = attend(q_two, blocks)
             span = slice(pair * rows, (pair + 1) * rows)
             t_ref[span, :] = y_ref[span, :] + jnp.where(seen, total, 0.0)
 
@@ -220,9 +223,11 @@
     def _():
         first = pick_ids(odd, low0, high0)[:, 0:1]
         q_two = pick(odd, low0, high0, pair * rows, rows).astype(jnp.bfloat16)
-        total = attend(q_two, mine[:rows, :], mine[rows : 2 * rows, :], own_ref[...] == first)
-        mask = pick_ids(odd, side0, side0) == first
-        o_ref[...] = total + attend(q_two, side[:rows, :], side[rows : 2 * rows, :], mask)
+        blocks = [
+            (mine[:rows, :], mine[rows : 2 * rows, :], own_ref[...] == first),
+            (side[:rows, :], side[rows : 2 * rows, :], pick_ids(odd, side0, side0) == first),
+        ]
+        o_ref[...] = attend(q_two, blocks)
 
 
 def far_body(stop, pair, high0, low0, side0, high, low, side, *refs):
@@ -237,8 +242,11 @@
         near_mask = pick_ids(odd, high0, low0) == first
         side_mask = jnp.where(odd, -1.0, pick_ids(odd, side0, side0)) == first
         q_two = pick(odd, low0, high0, pair * rows, rows).astype(jnp.bfloat16)
-        total = attend(q_two, *pick_pair(odd, [high], [low], 0, rows), near_mask)
-        total = total + attend(q_two, *pick_pair(odd, [side], [side], 0, rows), side_mask)
+        blocks = [
+            (*pick_pair(odd, [high], [low], 0, rows), near_mask),
+            (side[:rows, :], side[rows : 2 * rows, :], side_mask),
+        ]
+        total = attend(q_two, blocks)
         if len(refs) > 1:
             total = total + jnp.where(here // 2 == stop - 1, refs[0][...], 0.0)
         o_ref[...] = total
@@ -306,8 +314,8 @@
         + [pltpu.VMEM((1, rows), ids.dtype), pltpu.SemaphoreType.DMA((4,))],
     )
     highs, lows = [high, *rest], [low, *rest]
-    got_high = [snake(high, 1)]
-    got_low = [snake(low, 0)]
+    got_high = [snake(high, 1, 0)]
+    got_low = [snake(low, 0, 0)]
     got = each(lambda x: climb(x, 0, stop), [None, *rest])[1:]
     got_high, got_low = got_high + got, got_low + got
     side = each(trade, lows)
@@ -324,7 +332,7 @@
         args = (*lead, high_side[0], got_high[pair], got_low[pair], high_side[pair], *extra)
         body = functools.partial(far_body, stop, pair)
         far = call(body, f32(rows, LANES), 4 * one, *args)
-        if pair < pairs - 1:
+        if BACK[pair] == "C":
             back.append([(None, climb(far, 1, couples))])
         else:
             evens = exchange(far, 1)
@@ -378,6 +386,9 @@
     return partly
 
 
+BACK = 'CT'
+
+
 def solution(mesh):
     placed = P(("groups", "ctx"), ("heads", "rep"))
     return jax.shard_map(

time: 17.1 us -> 17.1 us (level)
  waiting for transfers between devices: 5.45 us -> 5.23 us
  transfers between devices with their start and end apart: 11 -> 11, of which waited for: 4 -> 4; matrix products, arithmetic and copies ran while one was open for 0% -> 0% of each run, Pallas kernels for 15% -> 16%
where the time goes in v6:
time: 17.1 us; the launch traced here: 16.9 us
  starting transfers between devices  7.88 us (46%)
  waiting for transfers between devices  5.23 us (31%)
  Pallas kernels  3.66 us (21%)
    pallas_call x9, Pallas kernels, call(): pl.pallas_call(body, out_shape=out, cost_estimate=pl.CostEstimate(flops=f...  3.66 us
    ppermute x5, starting transfers between devices, trade(): lax.ppermute(x, 'ctx', [(i, i ^ 1) for i in range(lax.axis_size('ctx'))])  3.44 us
    ppermute x2, waiting for transfers between devices, snake(): return lax.ppermute(x, 'ctx', pairs)  3.04 us
    ppermute x2, starting transfers between devices, climb(): return lax.ppermute(x, 'ctx', pairs)  2.51 us
    ppermute x2, waiting for transfers between devices, exchange(): return lax.ppermute(x, 'ctx', pairs)  2.06 us
    ppermute x2, starting transfers between devices, snake(): return lax.ppermute(x, 'ctx', pairs)  1.48 us
    ppermute x2, starting transfers between devices, exchange(): return lax.ppermute(x, 'ctx', pairs)  0.44 us
  transfers between devices with their start and end apart: 11, of which 4 were waited for; matrix products, arithmetic and copies ran while one was open for 0% of the time, Pallas kernels for 16%

profile of v6, /device:TPU:13, one launch (start us, length us, event | category | flops | bytes accessed | tf_op | source)
XLA Modules:
  0.0 16.9 jit_solution(13544967549141949555)
XLA Ops:
  0.0 1.0 %shard_map.46 = (f32[264,128]{1,0:T(8,128)S(1)}, f32[264,128]{1,0:T(8,128)S(1)}, f32[256,128]{1,0:T(8,128)S(1)}, f32[1,128]{1,0:T(1,128)S(1)}) custom-call(bf16[128,256]{1,0:T(8,128)(2,1)} %k_hbm.1, bf16[128,256]{1,0:T(8,128)(2,1)} %v_hbm.1, bf16[128,256]{1,0:T(8,128)(2,1)} %q_ref.3, s32[1,128]{1,0:T(1,128)} %bitcast.1), custom_call_target="tpu_custom_call" | custom-call | bytes 197120 | tf_op jit(solution)/shard_map/pallas_call | solution.py:274
  1.0 1.3 %collective-permute-start.2 = (f32[264,128]{1,0:T(8,128)S(1)}, f32[264,128]{1,0:T(8,128)S(1)}, u32[]{:S(2)}, u32[]{:S(2)}) collective-permute-start(f32[264,128]{1,0:T(8,128)S(1)} %get-tuple-element.14.refs_0_), channel_id=1, source_target_pairs={{2,6},{0,2},{6,10},{4,0},{10,14},{8,4},{14,12},{12,8},{3,7},{1,3},... | collective-permute-start | bytes 405512 | tf_op jit(solution)/shard_map/ppermute | solution.py:26
  2.3 1.3 %collective-permute-start.3 = (f32[256,128]{1,0:T(8,128)S(1)}, f32[256,128]{1,0:T(8,128)S(1)}, u32[]{:S(2)}, u32[]{:S(2)}) collective-permute-start(f32[256,128]{1,0:T(8,128)S(1)} %get-tuple-element.15.refs_1_.refs_3_.mine), channel_id=1, source_target_pairs={{0,4},{2,6},{4,8},{6,10},{8,0},{10,2},{12,14},{14,12},{1,5},{3,7},... | collective-permute-start | bytes 393224 | tf_op jit(solution)/shard_map/ppermute | solution.py:36
  3.6 0.2 %collective-permute-start.4 = (f32[264,128]{1,0:T(8,128)S(1)}, f32[264,128]{1,0:T(8,128)S(1)}, u32[]{:S(2)}, u32[]{:S(2)}) collective-permute-start(f32[264,128]{1,0:T(8,128)S(1)} %get-tuple-element.16.refs_2_), channel_id=1, source_target_pairs={{0,4},{2,0},{4,8},{6,2},{8,12},{10,6},{12,14},{14,10},{1,5},{3,1},... | collective-permute-start | bytes 405512 | tf_op jit(solution)/shard_map/ppermute | solution.py:26
  3.8 0.0 collective-permute-start
  3.8 1.4 %collective-permute-done.2.refs_0_.high0.high = f32[264,128]{1,0:T(8,128)S(1)} collective-permute-done((f32[264,128]{1,0:T(8,128)S(1)}, f32[264,128]{1,0:T(8,128)S(1)}, u32[]{:S(2)}, u32[]{:S(2)}) %collective-permute-start.2) | collective-permute-done | bytes 135200 | tf_op jit(solution)/shard_map/ppermute | solution.py:26
  5.2 2.9 %collective-permute-start.5 = (f32[264,128]{1,0:T(8,128)S(1)}, f32[264,128]{1,0:T(8,128)S(1)}, u32[]{:S(2)}, u32[]{:S(2)}) collective-permute-start(f32[264,128]{1,0:T(8,128)S(1)} %collective-permute-done.2.refs_0_.high0.high), channel_id=1, source_target_pairs={{0,2},{2,0},{4,6},{6,4},{8,10},{10,8},{12,14},{14,12},{1,3},{3,1},... | collective-permute-start | bytes 405512 | tf_op jit(solution)/shard_map/ppermute | solution.py:51
  8.1 0.0 collective-permute-start.1
  8.1 0.0 collective-permute-done.3.refs_1_.refs_3_.high.low
  8.1 0.5 %collective-permute-start.6 = (f32[256,128]{1,0:T(8,128)S(1)}, f32[256,128]{1,0:T(8,128)S(1)}, u32[]{:S(2)}, u32[]{:S(2)}) collective-permute-start(f32[256,128]{1,0:T(8,128)S(1)} %collective-permute-done.3.refs_1_.refs_3_.high.low), channel_id=1, source_target_pairs={{0,2},{2,0},{4,6},{6,4},{8,10},{10,8},{12,14},{14,12},{1,3},{3,1},... | collective-permute-start | bytes 393224 | tf_op jit(solution)/shard_map/ppermute | solution.py:51
  8.6 1.7 %collective-permute-done.4.refs_2_.low0.low = f32[264,128]{1,0:T(8,128)S(1)} collective-permute-done((f32[264,128]{1,0:T(8,128)S(1)}, f32[264,128]{1,0:T(8,128)S(1)}, u32[]{:S(2)}, u32[]{:S(2)}) %collective-permute-start.4) | collective-permute-done | bytes 135200 | tf_op jit(solution)/shard_map/ppermute | solution.py:26
  10.2 0.0 collective-permute-start.7
  10.3 0.0 collective-permute-done.1.refs_5_.side
  10.3 0.0 collective-permute-done.refs_4_.side0
  10.3 0.0 collective-permute-done.5.refs_4_.side0.side
  10.3 0.4 %shard_map.49 = f32[128,128]{1,0:T(8,128)S(1)} custom-call(f32[264,128]{1,0:T(8,128)S(1)} %collective-permute-done.2.refs_0_.high0.high, f32[264,128]{1,0:T(8,128)S(1)} %collective-permute-done.4.refs_2_.low0.low, f32[264,128]{1,0:T(8,128)S(1)} %collective-permute-done.5.refs_4_.side0.side, f32[264,128]{1,0:T(8,128)S(1)} %collective-permute-done.2.refs_0_.high0.high, ...), custom_call_target="tpu_custom_call" | custom-call | flops 33554432 | bytes 811008 | tf_op jit(solution)/shard_map/pallas_call | solution.py:274
  10.7 0.0 copy-start
  10.7 1.2 %collective-permute-start.8 = (f32[128,128]{1,0:T(8,128)S(1)}, f32[128,128]{1,0:T(8,128)S(1)}, u32[]{:S(2)}, u32[]{:S(2)}) collective-permute-start(f32[128,128]{1,0:T(8,128)S(1)} %shard_map.49), channel_id=1, source_target_pairs={{0,2},{2,0},{4,8},{6,10},{8,12},{10,14},{12,4},{14,6},{1,3},{3,1},... | collective-permute-start | bytes 196616 | tf_op jit(solution)/shard_map/ppermute | solution.py:36
  11.9 0.0 collective-permute-done.6.refs_5_.refs_7_.side
  11.9 0.3 %shard_map.52 = f32[128,128]{1,0:T(8,128)S(1)} custom-call(f32[264,128]{1,0:T(8,128)S(1)} %collective-permute-done.2.refs_0_.high0.high, f32[264,128]{1,0:T(8,128)S(1)} %collective-permute-done.4.refs_2_.low0.low, f32[264,128]{1,0:T(8,128)S(1)} %collective-permute-done.5.refs_4_.side0.side, f32[256,128]{1,0:T(8,128)S(1)} %collective-permute-done.3.refs_1_.refs_3_.high.low, ...), custom_call_target="tpu_custom_call" | custom-call | flops 33554432 | bytes 864256 | tf_op jit(solution)/shard_map/pallas_call | solution.py:274
  12.3 0.1 collective-permute-start.9
  12.4 0.3 %collective-permute-start.10 = (f32[128,128]{1,0:T(8,128)S(1)}, f32[128,128]{1,0:T(8,128)S(1)}, u32[]{:S(2)}, u32[]{:S(2)}) collective-permute-start(f32[128,128]{1,0:T(8,128)S(1)} %shard_map.52), channel_id=1, source_target_pairs={{0,2},{2,0},{4,6},{6,4},{8,12},{10,14},{12,8},{14,10},{1,3},{3,1},... | collective-permute-start | bytes 196616 | tf_op jit(solution)/shard_map/ppermute | solution.py:47
  12.7 0.0 copy-done
  12.7 0.6 %shard_map.47 = (f32[256,128]{1,0:T(8,128)S(1)}, bf16[128,256]{1,0:T(8,128)(2,1)}) custom-call(bf16[128,256]{1,0:T(8,128)(2,1)S(1)} %copy-done, f32[264,128]{1,0:T(8,128)S(1)} %get-tuple-element.14.refs_0_, f32[256,128]{1,0:T(8,128)S(1)} %get-tuple-element.15.refs_1_.refs_3_.mine, f32[264,128]{1,0:T(8,128)S(1)} %get-tuple-element.16.refs_2_, ...), custom_call_target="tpu_custom_call" | custom-call | flops 67108864 | bytes 864256 | tf_op jit(solution)/shard_map/pallas_call | solution.py:274
  13.3 0.0 collective-permute-done.7.refs_6_
  13.3 1.4 %shard_map.48 = (f32[256,128]{1,0:T(8,128)S(1)}, bf16[128,256]{1,0:T(8,128)(2,1)}) custom-call(bf16[128,256]{1,0:T(8,128)(2,1)S(1)} %copy-done, f32[1,128]{1,0:T(1,128)S(1)} %get-tuple-element.13.own_ref, f32[256,128]{1,0:T(8,128)S(1)} %get-tuple-element.17.y_ref, bf16[128,256]{1,0:T(8,128)(2,1)} %get-tuple-element.18._, ...), custom_call_target="tpu_custom_call", output_to_operand_aliasing={{1}: (3, {})} | custom-call | flops 67108864 | bytes 1327616 | tf_op jit(solution)/shard_map/pallas_call | solution.py:274
  14.6 0.1 collective-permute-done.8.came
  14.8 2.1 %collective-permute-done.9.came = f32[128,128]{1,0:T(8,128)S(1)} collective-permute-done((f32[128,128]{1,0:T(8,128)S(1)}, f32[128,128]{1,0:T(8,128)S(1)}, u32[]{:S(2)}, u32[]{:S(2)}) %collective-permute-start.9) | collective-permute-done | bytes 65568 | tf_op jit(solution)/shard_map/ppermute | solution.py:47
  16.8 0.0 collective-permute-done.10.came
  (4 shorter events, 0.1 us)
Async XLA Ops:
  1.0 4.2 %collective-permute-start.2 = (f32[264,128]{1,0:T(8,128)S(1)}, f32[264,128]{1,0:T(8,128)S(1)}, u32[]{:S(2)}, u32[]{:S(2)}) collective-permute-start(f32[264,128]{1,0:T(8,128)S(1)} %get-tuple-element.14.refs_0_), channel_id=1, source_target_pairs={{2,6},{0,2},{6,10},{4,0},{10,14},{8,4},{14,12},{12,8},{3,7},{1,3},... | collective-permute-start | bytes 405512 | tf_op jit(solution)/shard_map/ppermute | solution.py:26
  2.3 5.8 %collective-permute-start.3 = (f32[256,128]{1,0:T(8,128)S(1)}, f32[256,128]{1,0:T(8,128)S(1)}, u32[]{:S(2)}, u32[]{:S(2)}) collective-permute-start(f32[256,128]{1,0:T(8,128)S(1)} %get-tuple-element.15.refs_1_.refs_3_.mine), channel_id=1, source_target_pairs={{0,4},{2,6},{4,8},{6,10},{8,0},{10,2},{12,14},{14,12},{1,5},{3,7},... | collective-permute-start | bytes 393224 | tf_op jit(solution)/shard_map/ppermute | solution.py:36
  3.6 6.7 %collective-permute-start.4 = (f32[264,128]{1,0:T(8,128)S(1)}, f32[264,128]{1,0:T(8,128)S(1)}, u32[]{:S(2)}, u32[]{:S(2)}) collective-permute-start(f32[264,128]{1,0:T(8,128)S(1)} %get-tuple-element.16.refs_2_), channel_id=1, source_target_pairs={{0,4},{2,0},{4,8},{6,2},{8,12},{10,6},{12,14},{14,10},{1,5},{3,1},... | collective-permute-start | bytes 405512 | tf_op jit(solution)/shard_map/ppermute | solution.py:26
  3.8 6.5 %collective-permute-start = (f32[264,128]{1,0:T(8,128)S(1)}, f32[264,128]{1,0:T(8,128)S(1)}, u32[]{:S(2)}, u32[]{:S(2)}) collective-permute-start(f32[264,128]{1,0:T(8,128)S(1)} %get-tuple-element.16.refs_2_), channel_id=1, source_target_pairs={{0,2},{2,0},{4,6},{6,4},{8,10},{10,8},{12,14},{14,12},{1,3},{3,1},... | collective-permute-start | bytes 405512 | tf_op jit(solution)/shard_map/ppermute | solution.py:51
  5.2 5.1 %collective-permute-start.5 = (f32[264,128]{1,0:T(8,128)S(1)}, f32[264,128]{1,0:T(8,128)S(1)}, u32[]{:S(2)}, u32[]{:S(2)}) collective-permute-start(f32[264,128]{1,0:T(8,128)S(1)} %collective-permute-done.2.refs_0_.high0.high), channel_id=1, source_target_pairs={{0,2},{2,0},{4,6},{6,4},{8,10},{10,8},{12,14},{14,12},{1,3},{3,1},... | collective-permute-start | bytes 405512 | tf_op jit(solution)/shard_map/ppermute | solution.py:51
  8.1 2.2 %collective-permute-start.1 = (f32[256,128]{1,0:T(8,128)S(1)}, f32[256,128]{1,0:T(8,128)S(1)}, u32[]{:S(2)}, u32[]{:S(2)}) collective-permute-start(f32[256,128]{1,0:T(8,128)S(1)} %get-tuple-element.15.refs_1_.refs_3_.mine), channel_id=1, source_target_pairs={{0,2},{2,0},{4,6},{6,4},{8,10},{10,8},{12,14},{14,12},{1,3},{3,1},... | collective-permute-start | bytes 393224 | tf_op jit(solution)/shard_map/ppermute | solution.py:51
  8.1 3.8 %collective-permute-start.6 = (f32[256,128]{1,0:T(8,128)S(1)}, f32[256,128]{1,0:T(8,128)S(1)}, u32[]{:S(2)}, u32[]{:S(2)}) collective-permute-start(f32[256,128]{1,0:T(8,128)S(1)} %collective-permute-done.3.refs_1_.refs_3_.high.low), channel_id=1, source_target_pairs={{0,2},{2,0},{4,6},{6,4},{8,10},{10,8},{12,14},{14,12},{1,3},{3,1},... | collective-permute-start | bytes 393224 | tf_op jit(solution)/shard_map/ppermute | solution.py:51
  10.2 3.0 %collective-permute-start.7 = (f32[264,128]{1,0:T(8,128)S(1)}, f32[264,128]{1,0:T(8,128)S(1)}, u32[]{:S(2)}, u32[]{:S(2)}) collective-permute-start(f32[264,128]{1,0:T(8,128)S(1)} %collective-permute-done.4.refs_2_.low0.low), channel_id=1, source_target_pairs={{0,2},{2,0},{4,6},{6,4},{8,10},{10,8},{12,14},{14,12},{1,3},{3,1},... | collective-permute-start | bytes 405512 | tf_op jit(solution)/shard_map/ppermute | solution.py:51
  10.7 2.0 %copy-start = (bf16[128,256]{1,0:T(8,128)(2,1)S(1)}, bf16[128,256]{1,0:T(8,128)(2,1)}, u32[]{:S(2)}) copy-start(bf16[128,256]{1,0:T(8,128)(2,1)} %q_ref.3) | copy-start | bytes 196612
  10.7 4.1 %collective-permute-start.8 = (f32[128,128]{1,0:T(8,128)S(1)}, f32[128,128]{1,0:T(8,128)S(1)}, u32[]{:S(2)}, u32[]{:S(2)}) collective-permute-start(f32[128,128]{1,0:T(8,128)S(1)} %shard_map.49), channel_id=1, source_target_pairs={{0,2},{2,0},{4,8},{6,10},{8,12},{10,14},{12,4},{14,6},{1,3},{3,1},... | collective-permute-start | bytes 196616 | tf_op jit(solution)/shard_map/ppermute | solution.py:36
  12.3 4.6 %collective-permute-start.9 = (f32[128,128]{1,0:T(8,128)S(1)}, f32[128,128]{1,0:T(8,128)S(1)}, u32[]{:S(2)}, u32[]{:S(2)}) collective-permute-start(f32[128,128]{1,0:T(8,128)S(1)} %shard_map.52), channel_id=1, source_target_pairs={{0,2},{2,0},{4,8},{6,10},{8,4},{10,6},{12,14},{14,12},{1,3},{3,1},... | collective-permute-start | bytes 196616 | tf_op jit(solution)/shard_map/ppermute | solution.py:47
  12.4 4.5 %collective-permute-start.10 = (f32[128,128]{1,0:T(8,128)S(1)}, f32[128,128]{1,0:T(8,128)S(1)}, u32[]{:S(2)}, u32[]{:S(2)}) collective-permute-start(f32[128,128]{1,0:T(8,128)S(1)} %shard_map.52), channel_id=1, source_target_pairs={{0,2},{2,0},{4,6},{6,4},{8,12},{10,14},{12,8},{14,10},{1,3},{3,1},... | collective-permute-start | bytes 196616 | tf_op jit(solution)/shard_map/ppermute | solution.py:47
